TPU v7x, 512 devices: a whole 4x8x8 slice. The times are simulated.
512 devices in a mesh: dp: 32 (over z, x), tensor: 16 (over y, core).
Axes of the slice: x: 4, y: 8, z: 8, core: 2. Of those that a mesh axis runs over, the one named last changes fastest.
Arguments:
- hidden: bfloat16 [8192, 2, 8192], P('dp', None, 'tensor'), may hold values from -6 to 6
- key_value_weight: bfloat16 [8192, 2048], P('tensor'), may hold values from -0.0625 to 0.0625
- adapter_down_weight: bfloat16 [512, 8192, 64], P('dp', 'tensor'), may hold values from -0.0625 to 0.0625
- adapter_up_weight: bfloat16 [512, 64, 2048], P('dp', None, 'tensor'), may hold values from -0.75 to 0.75
- attempt_adapter_slot: int32 [8192, 1], P('dp'), may hold values from 0 to 31; in each aligned block of 256 rows (0 to 255, 256 to 511, ...) at most 32 rows name the same one
- group_slot_task: int32 [32, 32], replicated, may hold values from 0 to 511, as said below
- task_row_position: int32 [512], replicated, may hold values from 0 to 511, as said below
- scores: int32 [8192], P('dp'), may hold values 0 or 1
- cotangent: bfloat16 [8192, 2, 2048], P('dp', None, 'tensor'), may hold values from -6 to 6
Outputs:
- kv_new: bfloat16 [8192, 2, 2048], P('dp', None, 'tensor')
- grad_down: bfloat16 [512, 8192, 64], P('dp', 'tensor')
- grad_up: bfloat16 [512, 64, 2048], P('dp', None, 'tensor')
Inputs may be any that keep to these rules, and one draw needn't show every extreme that they name: `attempt_adapter_slot`: among the 256 attempts of one group (aligned blocks of 256 rows), at most 32 name the same slot, and exactly 32 do in some block. `task_row_position`: every row is named once; rows o * 16 to (o + 1) * 16 - 1 belong to group o. group_slot_task[g, o] is a task t with task_row_position[t] between o * 16 and (o + 1) * 16 - 1.
All inputs are finite; a program needn't handle non-finite values. No bound on the sum of `scores` on one device may be relied on, other than what follows from the above.
Results may differ from a plain program's by a relative error of at most 0.0057.
Values may be sent and summed in bfloat16 or wider, within the bound.
A program may use at most 64 MiB of HBM per device.

v0:
```python
import jax
import jax.numpy as jnp
from jax import lax
from jax.sharding import PartitionSpec as P

adapter_output_scale = 0.25
precise = lax.Precision.HIGHEST


def rank_totals(down_part, back_part):
    return lax.psum((down_part, back_part), "tensor")


def body(
    hidden,
    key_value_weight,
    adapter_down_weight,
    adapter_up_weight,
    attempt_adapter_slot,
    group_slot_task,
    task_row_position,
    scores,
    cotangent,
):
    group_total = lax.axis_size("dp")
    my_group = lax.axis_index("dp")
    att_rows, step_count, width_part = hidden.shape
    task_on_device = adapter_down_weight.shape[0]
    tasks_all = task_row_position.shape[0]
    kv_part = cotangent.shape[2]
    row_count = att_rows * step_count
    slot_ids = jnp.arange(group_total, dtype=jnp.int32)
    slot_of = attempt_adapter_slot[:, 0]
    slot_hot = slot_of[:, None] == slot_ids[None, :]
    my_tasks = lax.dynamic_index_in_dim(group_slot_task, my_group, 0, keepdims=False)
    task_of = jnp.sum(jnp.where(slot_hot, my_tasks[None, :], 0), axis=1)
    task_ids = jnp.arange(tasks_all, dtype=jnp.int32)
    task_hot = (task_of[:, None] == task_ids[None, :]).astype(jnp.float32)
    score_f = scores.astype(jnp.float32)
    sums_local = jnp.dot(score_f, task_hot, precision=precise)
    counts_local = jnp.sum(task_hot, axis=0)
    score_sums, task_counts = lax.psum((sums_local, counts_local), "dp")
    task_means = score_sums / jnp.maximum(task_counts, 1.0)
    advantage = score_f - jnp.dot(task_hot, task_means, precision=precise)
    weighted = (advantage[:, None, None] * cotangent.astype(jnp.float32)).astype(jnp.bfloat16)
    served = lax.dynamic_index_in_dim(group_slot_task, my_group, 1, keepdims=False)
    stored = jnp.sum(
        jnp.where(served[:, None] == task_ids[None, :], task_row_position[None, :], 0), axis=1
    )
    slot_on_device = stored % task_on_device
    picker = (
        slot_on_device[:, None] == jnp.arange(task_on_device, dtype=jnp.int32)[None, :]
    ).astype(jnp.float32)
    flat_rows = hidden.reshape(row_count, width_part)
    base_terms = jnp.dot(flat_rows, key_value_weight, preferred_element_type=jnp.float32)
    base_rows = lax.psum_scatter(base_terms, "tensor", scatter_dimension=1, tiled=True)
    weighted_rows = weighted.reshape(row_count, kv_part)
    outgoing_down_weight = jnp.take(adapter_down_weight, slot_on_device, axis=0)
    outgoing_up_weight = jnp.take(adapter_up_weight, slot_on_device, axis=0)
    got_down, got_up = (
        lax.all_to_all(outgoing_down_weight, "dp", split_axis=0, concat_axis=0, tiled=True),
        lax.all_to_all(outgoing_up_weight, "dp", split_axis=0, concat_axis=0, tiled=True),
    )
    row_hot = jnp.repeat(slot_hot, step_count, axis=0)
    row_mask = row_hot.astype(jnp.float32)
    down_all = jnp.einsum("nd,sdr->nsr", flat_rows, got_down, preferred_element_type=jnp.float32)
    back_all = jnp.einsum("nk,srk->nsr", weighted_rows, got_up, preferred_element_type=jnp.float32)
    down_part = jnp.sum(down_all * row_mask[:, :, None], axis=1)
    back_part = jnp.sum(back_all * row_mask[:, :, None], axis=1)
    down_total, back_total = rank_totals(down_part, back_part)
    zero_bf = jnp.zeros((), jnp.bfloat16)
    down_spread = jnp.where(
        row_hot[:, :, None], down_total.astype(jnp.bfloat16)[:, None, :], zero_bf
    )
    back_spread = jnp.where(
        row_hot[:, :, None], back_total.astype(jnp.bfloat16)[:, None, :], zero_bf
    )
    adapter_delta_rows = (
        adapter_output_scale
        * jnp.einsum("nsr,srk->nk", down_spread, got_up, preferred_element_type=jnp.float32)
    ).astype(jnp.bfloat16)
    down_gradient_sender = adapter_output_scale * jnp.einsum(
        "nd,nsr->sdr", flat_rows, back_spread, preferred_element_type=jnp.float32
    )
    up_gradient_sender = adapter_output_scale * jnp.einsum(
        "nsr,nk->srk", down_spread, weighted_rows, preferred_element_type=jnp.float32
    )
    got_grad_down, got_grad_up = (
        lax.all_to_all(down_gradient_sender, "dp", split_axis=0, concat_axis=0, tiled=True),
        lax.all_to_all(up_gradient_sender, "dp", split_axis=0, concat_axis=0, tiled=True),
    )
    kv_new = (base_rows + adapter_delta_rows.astype(jnp.float32)).astype(jnp.bfloat16)
    kv_new = kv_new.reshape(att_rows, step_count, kv_part)
    grad_down = jnp.einsum("st,sdr->tdr", picker, got_grad_down, precision=precise).astype(
        jnp.bfloat16
    )
    grad_up = jnp.einsum("st,srk->trk", picker, got_grad_up, precision=precise).astype(jnp.bfloat16)
    return (kv_new, grad_down, grad_up)


def solution(mesh):
    in_specs = (
        P("dp", None, "tensor"),
        P("tensor", None),
        P("dp", "tensor", None),
        P("dp", None, "tensor"),
        P("dp", None),
        P(),
        P(),
        P("dp"),
        P("dp", None, "tensor"),
    )
    out_specs = (P("dp", None, "tensor"), P("dp", "tensor", None), P("dp", None, "tensor"))
    return jax.shard_map(body, mesh=mesh, in_specs=in_specs, out_specs=out_specs, check_vma=False)
```

profile of v0, /device:TPU:6, one launch (start us, length us, event | category | flops | bytes accessed | tf_op | source)
XLA Modules:
  0.0 361.3 jit_solution(851821067383386259)
XLA Ops:
  9.7 2.4 gather_fusion.1
  12.0 2.0 broadcast_select_fusion.1
  14.0 13.5 %all-to-all-start.1 = ((bf16[32,64,128]{2,1,0:T(8,128)(2,1)}), bf16[32,64,128]{2,1,0:T(8,128)(2,1)}, u32[]{:S(2)}, u32[]{:S(2)}) async-start(bf16[32,64,128]{2,1,0:T(8,128)(2,1)} %broadcast_select_fusion.1), calls=%async_computation.2 | async-start | bytes 1048576 | tf_op jit(solution)/shard_map/all_to_all | solution.py:62
  27.5 2.0 gather_fusion
  29.4 3.1 broadcast_select_fusion
  32.6 11.8 %all-to-all-done.1 = bf16[32,64,128]{2,1,0:T(8,128)(2,1)} async-done(((bf16[32,64,128]{2,1,0:T(8,128)(2,1)}), bf16[32,64,128]{2,1,0:T(8,128)(2,1)}, u32[]{:S(2)}, u32[]{:S(2)}) %all-to-all-start.1) | async-done | bytes 524320 | tf_op jit(solution)/shard_map/all_to_all | solution.py:62
  44.3 5.6 %all-to-all-start = ((bf16[32,512,64]{1,2,0:T(8,128)(2,1)}), bf16[32,512,64]{1,2,0:T(8,128)(2,1)}, u32[]{:S(2)}, u32[]{:S(2)}) async-start(bf16[32,512,64]{1,2,0:T(8,128)(2,1)} %broadcast_select_fusion), calls=%async_computation.1 | async-start | bytes 4194304 | tf_op jit(solution)/shard_map/all_to_all | solution.py:61
  53.6 101.0 %all-reduce = (f32[512]{0:T(512)S(1)}, f32[512]{0:T(512)S(1)}) all-reduce(f32[512]{0:T(512)S(1)} %bitcast.52, f32[512]{0:T(512)S(1)} %convert_reduce_fusion), channel_id=1, replica_groups=mesh['dp'=32,'tensor'=16] {'dp'}, use_global_device_ids=true, to_apply=%region_5.6 | all-reduce | flops 1024 | bytes 8192 | tf_op jit(solution)/shard_map/psum | solution.py:42
  156.0 1.8 multiply_reduce_fusion
  157.8 2.9 fusion
  160.7 48.6 %all-reduce.3 = (bf16[512,64]{0,1:T(8,128)(2,1)S(1)}, bf16[512,64]{0,1:T(8,128)(2,1)S(1)}) all-reduce(f32[512,64]{0,1:T(8,128)S(1)} %fusion, f32[512,64]{0,1:T(8,128)S(1)} %multiply_reduce_fusion), channel_id=1, replica_groups=mesh['dp'=32,'tensor'=16] {'tensor'}, use_global_device_ids=true, to_apply=%region_3.4 | all-reduce | flops 65536 | bytes 393216 | tf_op jit(solution)/shard_map/psum | solution.py:11
  210.0 1.6 copy.51
  211.6 13.7 %all-to-all-start.3 = ((f32[32,64,128]{2,1,0:T(8,128)}), f32[32,64,128]{2,1,0:T(8,128)S(1)}, u32[]{:S(2)}, u32[]{:S(2)}) async-start(f32[32,64,128]{2,1,0:T(8,128)} %copy.51), calls=%async_computation.4 | async-start | bytes 2097152 | tf_op jit(solution)/shard_map/all_to_all | solution.py:90
  225.6 2.1 reshape.80
  227.7 4.2 %fusion.58 = f32[512,2048]{1,0:T(8,128)} fusion(bf16[512,512]{1,0:T(8,128)(2,1)} %reshape.80, bf16[512,2048]{1,0:T(8,128)(2,1)S(1)} %copy-done), kind=kOutput, calls=%fused_computation.70 | convolution fusion | flops 1073741824 | bytes 6815744 | tf_op jit(solution)/shard_map/dot_general | solution.py:55
  231.9 2.3 multiply_bitcast_fusion
  234.2 4.4 %copy.49 = f32[32,512,64]{1,2,0:T(8,128)} copy(f32[32,512,64]{1,0,2:T(8,128)S(1)} %multiply_bitcast_fusion) | data formatting | bytes 8388608 | tf_op jit(solution)/shard_map/mul | solution.py:82
  238.6 11.6 %all-to-all-done.3 = f32[32,64,128]{2,1,0:T(8,128)S(1)} async-done(((f32[32,64,128]{2,1,0:T(8,128)}), f32[32,64,128]{2,1,0:T(8,128)S(1)}, u32[]{:S(2)}, u32[]{:S(2)}) %all-to-all-start.3) | async-done | bytes 1048608 | tf_op jit(solution)/shard_map/all_to_all | solution.py:90
  250.2 6.0 %all-to-all-start.2 = ((f32[32,512,64]{1,2,0:T(8,128)}), f32[32,512,64]{1,2,0:T(8,128)}, u32[]{:S(2)}, u32[]{:S(2)}) async-start(f32[32,512,64]{1,2,0:T(8,128)} %copy.49), calls=%async_computation.3 | async-start | bytes 8388608 | tf_op jit(solution)/shard_map/all_to_all | solution.py:89
  258.0 41.2 %reduce-scatter.2.cloned.1.call-done = f32[512,128]{1,0:T(8,128)} async-done(((f32[512,2048]{1,0:T(8,128)}), f32[512,128]{1,0:T(8,128)}) %reduce-scatter.2.cloned.1.call-update) | async-done | bytes 262160 | tf_op jit(solution)/shard_map/reduce_scatter | solution.py:56
  299.2 2.6 fusion.32
  301.8 45.2 %all-to-all-done.2 = f32[32,512,64]{1,2,0:T(8,128)} async-done(((f32[32,512,64]{1,2,0:T(8,128)}), f32[32,512,64]{1,2,0:T(8,128)}, u32[]{:S(2)}, u32[]{:S(2)}) %all-to-all-start.2) | async-done | bytes 4194336 | tf_op jit(solution)/shard_map/all_to_all | solution.py:89
  347.0 5.9 %fusion.11 = bf16[16,512,64]{1,0,2:T(8,128)(2,1)S(1)} fusion(f32[32,512,64]{1,2,0:T(8,128)} %all-to-all-done.2, s32[32]{0:T(128)S(1)} %copy-done.6), kind=kOutput, calls=%fused_computation.17 | convolution fusion | flops 201851392 | bytes 5243008 | tf_op jit(solution)/shard_map/st,sdr->tdr/dot_general | solution.py:94
  352.9 1.5 copy.53
  (41 shorter events, 10.3 us)
Async XLA Ops:
  7.2 220.5 %copy-start = (bf16[512,2048]{1,0:T(8,128)(2,1)S(1)}, bf16[512,2048]{1,0:T(8,128)(2,1)}, u32[]{:S(2)}) copy-start(bf16[512,2048]{1,0:T(8,128)(2,1)} %param.10) | copy-start | bytes 6291460
  7.2 20.3 %copy-start.1 = (bf16[16,512,64]{1,2,0:T(8,128)(2,1)S(1)}, bf16[16,512,64]{1,2,0:T(8,128)(2,1)}, u32[]{:S(2)}) copy-start(bf16[16,512,64]{1,2,0:T(8,128)(2,1)} %param.11) | copy-start | bytes 3145732
  14.0 30.4 %all-to-all-start.1 = ((bf16[32,64,128]{2,1,0:T(8,128)(2,1)}), bf16[32,64,128]{2,1,0:T(8,128)(2,1)}, u32[]{:S(2)}, u32[]{:S(2)}) async-start(bf16[32,64,128]{2,1,0:T(8,128)(2,1)} %broadcast_select_fusion.1), calls=%async_computation.2 | async-start | bytes 1048576 | tf_op jit(solution)/shard_map/all_to_all | solution.py:62
  32.6 17.4 %copy-start.5 = (s32[256,1]{0,1:T(1,128)S(1)}, s32[256,1]{0,1:T(1,128)}, u32[]{:S(2)}) copy-start(s32[256,1]{0,1:T(1,128)} %param.13) | copy-start | bytes 3076
  32.6 18.0 %copy-start.2 = (bf16[256,2,512]{2,1,0:T(2,128)(2,1)S(1)}, bf16[256,2,512]{2,1,0:T(2,128)(2,1)}, u32[]{:S(2)}) copy-start(bf16[256,2,512]{2,1,0:T(2,128)(2,1)} %param.9) | copy-start | bytes 1572868
  44.3 113.5 %all-to-all-start = ((bf16[32,512,64]{1,2,0:T(8,128)(2,1)}), bf16[32,512,64]{1,2,0:T(8,128)(2,1)}, u32[]{:S(2)}, u32[]{:S(2)}) async-start(bf16[32,512,64]{1,2,0:T(8,128)(2,1)} %broadcast_select_fusion), calls=%async_computation.1 | async-start | bytes 4194304 | tf_op jit(solution)/shard_map/all_to_all | solution.py:61
  50.0 105.7 %copy-start.4 = (bf16[256,2,128]{2,1,0:T(2,128)(2,1)S(1)}, bf16[256,2,128]{2,1,0:T(2,128)(2,1)}, u32[]{:S(2)}) copy-start(bf16[256,2,128]{2,1,0:T(2,128)(2,1)} %param.17) | copy-start | bytes 393220
  50.8 107.1 %copy-start.3 = (bf16[512,512,1]{1,0,2:T(8,128)(2,1)}, bf16[512,512,1]{1,0,2:T(8,128)(2,1)S(1)}, u32[]{:S(2)}) copy-start(bf16[512,512,1]{1,0,2:T(8,128)(2,1)S(1)} %reshape.99) | copy-start | bytes 1572868
  211.6 38.6 %all-to-all-start.3 = ((f32[32,64,128]{2,1,0:T(8,128)}), f32[32,64,128]{2,1,0:T(8,128)S(1)}, u32[]{:S(2)}, u32[]{:S(2)}) async-start(f32[32,64,128]{2,1,0:T(8,128)} %copy.51), calls=%async_computation.4 | async-start | bytes 2097152 | tf_op jit(solution)/shard_map/all_to_all | solution.py:90
  225.4 73.8 %reduce-scatter.2.cloned.1.call-start = ((), (), s32[]{:S(2)}) async-start(), calls=%async_computation.5 | async-start | bytes 4456448 | tf_op jit(solution)/shard_map/reduce_scatter | solution.py:56
  238.6 17.5 %copy-start.6 = (s32[32]{0:T(128)S(1)}, s32[32]{0:T(128)}, u32[]{:S(2)}) copy-start(s32[32]{0:T(128)} %get-tuple-element.26) | copy-start | bytes 388
  250.2 96.8 %all-to-all-start.2 = ((f32[32,512,64]{1,2,0:T(8,128)}), f32[32,512,64]{1,2,0:T(8,128)}, u32[]{:S(2)}, u32[]{:S(2)}) async-start(f32[32,512,64]{1,2,0:T(8,128)} %copy.49), calls=%async_computation.3 | async-start | bytes 8388608 | tf_op jit(solution)/shard_map/all_to_all | solution.py:89
Sparse Core Ops, SparseCore 0:
  232.0 67.1 reduce-scatter.1
where the time goes:
time: 368 us; the launch traced here: 361 us
  blocking collectives  150 us (41%)
  waiting for transfers between devices  110 us (30%)
  starting transfers between devices  39 us (11%)
  matrix products  22.2 us (6%)
  local copies, waits for them, and re-layouts  17.2 us (5%)
  between operations  14.3 us (4%)
  other arithmetic  9.39 us (3%)
    psum x1, blocking collectives, body(): score_sums, task_counts = lax.psum((sums_local, counts_local), 'dp')  101 us
    psum x1, blocking collectives, rank_totals(): return lax.psum((down_part, back_part), 'tensor')  48.6 us
    all_to_all x1, waiting for transfers between devices, body(): lax.all_to_all(down_gradient_sender, 'dp', split_axis=0, concat_axis=0, t...  45.2 us
    reduce_scatter x1, waiting for transfers between devices, body(): lax.psum_scatter(base_terms, 'tensor', scatter_dimension=1, tiled=True)  41.2 us
    all_to_all x1, starting transfers between devices, body(): lax.all_to_all(up_gradient_sender, 'dp', split_axis=0, concat_axis=0, til...  13.7 us
    all_to_all x1, starting transfers between devices, body(): lax.all_to_all(outgoing_up_weight, 'dp', split_axis=0, concat_axis=0, til...  13.5 us
    all_to_all x1, waiting for transfers between devices, body(): lax.all_to_all(outgoing_up_weight, 'dp', split_axis=0, concat_axis=0, til...  11.8 us
    all_to_all x1, waiting for transfers between devices, body(): lax.all_to_all(up_gradient_sender, 'dp', split_axis=0, concat_axis=0, til...  11.6 us
  transfers between devices with their start and end apart: 5, of which 4 were waited for; matrix products, arithmetic and copies ran while one was open for 8% of the time, Pallas kernels for 0%

commit v1 on v0

v1 whole, which is shorter than its diff:
```python
import jax
import jax.numpy as jnp
from jax import lax
from jax.sharding import PartitionSpec as P

adapter_output_scale = 0.25


def body(
    hidden,
    key_value_weight,
    adapter_down_weight,
    adapter_up_weight,
    attempt_adapter_slot,
    group_slot_task,
    task_row_position,
    scores,
    cotangent,
):
    groups = lax.axis_size("dp")
    me = lax.axis_index("dp")
    att, steps, width = hidden.shape
    task_dev, _, rank = adapter_down_weight.shape
    kv = cotangent.shape[2]
    most = att // 8
    bf16, f32 = jnp.bfloat16, jnp.float32
    slot = attempt_adapter_slot[:, 0]
    ids = jnp.arange(groups, dtype=jnp.int32)
    hot = slot[:, None] == ids[None, :]
    order = jnp.arange(att, dtype=jnp.int32)
    earlier = (order[:, None] > order[None, :]) & (slot[:, None] == slot[None, :])
    place = slot * most + jnp.sum(earlier.astype(jnp.int32), axis=1)
    pick = jnp.arange(groups * most, dtype=jnp.int32)[:, None] == place[None, :]
    pick_bf = pick.astype(bf16)
    hid_out = jnp.einsum("pa,asd->psd", pick_bf, hidden, preferred_element_type=f32).astype(bf16)
    cot_out = jnp.einsum("pa,ask->psk", pick_bf, cotangent, preferred_element_type=f32).astype(bf16)
    mark_out = jnp.sum(
        jnp.where(pick[:, None, :], jnp.stack([scores, jnp.ones_like(scores)])[None], 0), axis=2
    ).astype(f32)
    mark_out = mark_out.reshape(groups, most, 2)

    def swap(x):
        return lax.all_to_all(x, "dp", split_axis=0, concat_axis=0, tiled=True)

    marks = swap(mark_out)
    hid = swap(hid_out.reshape(groups, most, steps, width))
    cot = swap(cot_out.reshape(groups, most, steps, kv))
    base_terms = jnp.einsum("asd,dk->ask", hidden, key_value_weight, preferred_element_type=f32)
    base = lax.psum_scatter(base_terms, "tensor", scatter_dimension=2, tiled=True)

    task_of = lax.dynamic_index_in_dim(group_slot_task, me, 1, keepdims=False)
    task_ids = jnp.arange(task_row_position.shape[0], dtype=jnp.int32)
    stored = jnp.sum(
        jnp.where(task_of[:, None] == task_ids[None, :], task_row_position[None, :], 0), axis=1
    )
    local = stored % task_dev
    local_hot = local[:, None] == jnp.arange(task_dev, dtype=jnp.int32)[None, :]
    same = (local[:, None] == local[None, :]).astype(f32)
    sums = jnp.sum(same[:, :, None] * jnp.sum(marks, axis=1)[None], axis=1)
    mean = sums[:, 0] / jnp.maximum(sums[:, 1], 1.0)
    advantage = marks[:, :, 0] - mean[:, None] * marks[:, :, 1]
    weighted = (advantage[:, :, None, None] * cot.astype(f32)).astype(bf16)

    down = jnp.take(adapter_down_weight, local, axis=0)
    up = jnp.take(adapter_up_weight, local, axis=0)
    inner_down = jnp.einsum("gjsd,gdr->gjsr", hid, down, preferred_element_type=f32)
    inner_back = jnp.einsum("gjsk,grk->gjsr", weighted, up, preferred_element_type=f32)
    inner = lax.psum(jnp.concatenate([inner_down, inner_back], axis=3), "tensor").astype(bf16)
    inner_down, inner_back = inner[..., :rank], inner[..., rank:]
    delta = (
        adapter_output_scale
        * jnp.einsum("gjsr,grk->gjsk", inner_down, up, preferred_element_type=f32)
    ).astype(bf16)
    delta = swap(delta)
    spread = jnp.where(local_hot[:, None, None, :, None], inner_back[:, :, :, None, :], 0)
    grad_down = jnp.einsum("gjsd,gjstr->tdr", hid, spread, preferred_element_type=f32)
    spread = jnp.where(local_hot[:, None, None, :, None], inner_down[:, :, :, None, :], 0)
    grad_up = jnp.einsum("gjstr,gjsk->trk", spread, weighted, preferred_element_type=f32)
    grad_down = (adapter_output_scale * grad_down).astype(bf16)
    grad_up = (adapter_output_scale * grad_up).astype(bf16)
    mine = jnp.einsum(
        "pa,psk->ask", pick_bf, delta.reshape(groups * most, steps, kv), preferred_element_type=f32
    )
    return (base + mine).astype(bf16), grad_down, grad_up


def solution(mesh):
    in_specs = (
        P("dp", None, "tensor"),
        P("tensor", None),
        P("dp", "tensor", None),
        P("dp", None, "tensor"),
        P("dp", None),
        P(),
        P(),
        P("dp"),
        P("dp", None, "tensor"),
    )
    out_specs = (P("dp", None, "tensor"), P("dp", "tensor", None), P("dp", None, "tensor"))
    return jax.shard_map(
        body, mesh=mesh, in_specs=in_specs, out_specs=out_specs, check_vma=False
    )
```

time: 368 us -> 210 us (0.57)
  blocking collectives: 150 us -> 58.2 us
  waiting for transfers between devices: 110 us -> 63.4 us
  starting transfers between devices: 39 us -> 31.6 us
  other arithmetic: 9.39 us -> 2.78 us
  local copies, waits for them, and re-layouts: 17.2 us -> 10.7 us
    psum x2 -> x1, blocking collectives: 150 us -> 58.2 us  [body(): lax.psum(jnp.concatenate([inner_down, inner_back], axis=3), 'tensor')]
    reduce_scatter x1, waiting for transfers between devices: 41.2 us -> 0.02 us  [body(): lax.psum_scatter(base_terms, 'tensor', scatter_dimension=2, tiled=True)]
    all_to_all x4, starting transfers between devices: 38.8 us -> 31.5 us  [swap(): return lax.all_to_all(x, 'dp', split_axis=0, concat_axis=0, tiled=True)]
    mul x2 -> x0, local copies, waits for them, and re-layouts: 5.99 us -> none  [the longest x1 4.41 us: body(): adapter_output_scale * jnp.einsum('nd,nsr->sdr', flat_rows, back_spread,...]
    all_to_all x4, waiting for transfers between devices: 68.5 us -> 63.4 us  [swap(): return lax.all_to_all(x, 'dp', split_axis=0, concat_axis=0, tiled=True)]
    select_n x3 -> x1, other arithmetic: 5.1 us -> 0.01 us  [body(): down = jnp.take(adapter_down_weight, local, axis=0)]
    dot_general x10 -> x9, matrix products: 22.2 us -> 25.7 us  [the longest x1 7.05 us: body(): jnp.einsum('gjsd,gjstr->tdr', hid, spread, preferred_element_type=f32)]
  transfers between devices with their start and end apart: 5 -> 5, of which waited for: 4 -> 4; matrix products, arithmetic and copies ran while one was open for 8% -> 15% of each run, Pallas kernels for 0% -> 0%
where the time goes in v1:
time: 210 us; the launch traced here: 207 us
  waiting for transfers between devices  63.4 us (30%)
  blocking collectives  58.2 us (28%)
  starting transfers between devices  31.6 us (15%)
  matrix products  25.7 us (12%)
  between operations  14.3 us (7%)
  local copies, waits for them, and re-layouts  10.7 us (5%)
  other arithmetic  2.78 us (1%)
    all_to_all x4, waiting for transfers between devices, swap(): return lax.all_to_all(x, 'dp', split_axis=0, concat_axis=0, tiled=True)  63.4 us
    psum x1, blocking collectives, body(): lax.psum(jnp.concatenate([inner_down, inner_back], axis=3), 'tensor')  58.2 us
    all_to_all x4, starting transfers between devices, swap(): return lax.all_to_all(x, 'dp', split_axis=0, concat_axis=0, tiled=True)  31.5 us
    dot_general x1, matrix products, body(): jnp.einsum('gjsd,gjstr->tdr', hid, spread, preferred_element_type=f32)  7.05 us
    dot_general x1, matrix products, body(): jnp.einsum('gjstr,gjsk->trk', spread, weighted, preferred_element_type=f32)  4.87 us
    dot_general x1, matrix products, body(): jnp.einsum('asd,dk->ask', hidden, key_value_weight, preferred_element_typ...  4.22 us
  transfers between devices with their start and end apart: 5, of which 4 were waited for; matrix products, arithmetic and copies ran while one was open for 15% of the time, Pallas kernels for 0%

profile of v1, /device:TPU:6, one launch (start us, length us, event | category | flops | bytes accessed | tf_op | source)
XLA Modules:
  0.0 206.7 jit_solution(15004701261736432002)
XLA Ops:
  7.2 1.5 copy-done
  8.8 4.2 %fusion.14 = f32[256,2,2048]{2,0,1:T(8,128)} fusion(bf16[512,2048]{1,0:T(8,128)(2,1)S(1)} %copy-done, bf16[256,2,512]{2,1,0:T(2,128)(2,1)} %param.9), kind=kOutput, calls=%fused_computation.17 | convolution fusion | flops 1073741824 | bytes 6815744 | tf_op jit(solution)/shard_map/asd,dk->ask/dot_general | solution.py:48
  15.7 13.4 %all-to-all-start.1 = ((f32[32,32,2]{1,2,0:T(2,128)}), f32[32,32,2]{1,2,0:T(2,128)S(1)}, u32[]{:S(2)}, u32[]{:S(2)}) async-start(f32[32,32,2]{1,2,0:T(2,128)} %copy.63), calls=%async_computation.2 | async-start | bytes 65536 | tf_op jit(solution)/shard_map/all_to_all | solution.py:43
  29.7 0.9 copy.68
  30.6 6.7 %all-to-all-done.1 = f32[32,32,2]{1,2,0:T(2,128)S(1)} async-done(((f32[32,32,2]{1,2,0:T(2,128)}), f32[32,32,2]{1,2,0:T(2,128)S(1)}, u32[]{:S(2)}, u32[]{:S(2)}) %all-to-all-start.1) | async-done | bytes 8224 | tf_op jit(solution)/shard_map/all_to_all | solution.py:43
  37.3 6.1 %all-to-all-start.2 = ((bf16[32,32,2,128]{3,1,2,0:T(8,128)(2,1)}), bf16[32,32,2,128]{3,1,2,0:T(8,128)(2,1)}, u32[]{:S(2)}, u32[]{:S(2)}) async-start(bf16[32,32,2,128]{3,1,2,0:T(8,128)(2,1)} %copy.68), calls=%async_computation.3 | async-start | bytes 1048576 | tf_op jit(solution)/shard_map/all_to_all | solution.py:43
  43.4 0.8 convolution_convert_fusion
  44.3 1.6 copy.61
  45.9 13.4 %all-to-all-done.2 = bf16[32,32,2,128]{3,1,2,0:T(8,128)(2,1)} async-done(((bf16[32,32,2,128]{3,1,2,0:T(8,128)(2,1)}), bf16[32,32,2,128]{3,1,2,0:T(8,128)(2,1)}, u32[]{:S(2)}, u32[]{:S(2)}) %all-to-all-start.2) | async-done | bytes 524320 | tf_op jit(solution)/shard_map/all_to_all | solution.py:43
  59.2 6.0 %all-to-all-start = ((bf16[32,32,2,512]{3,1,2,0:T(8,128)(2,1)}), bf16[32,32,2,512]{3,1,2,0:T(8,128)(2,1)}, u32[]{:S(2)}, u32[]{:S(2)}) async-start(bf16[32,32,2,512]{3,1,2,0:T(8,128)(2,1)} %copy.61), calls=%async_computation.1 | async-start | bytes 4194304 | tf_op jit(solution)/shard_map/all_to_all | solution.py:43
  65.7 1.4 gather_fusion.1
  67.1 2.1 %gather_fusion = bf16[32,512,64]{1,2,0:T(8,128)(2,1)} fusion(bf16[16,512,64]{1,2,0:T(8,128)(2,1)S(1)} %copy-done.1, s32[1024]{0:T(1024)S(1)} %pad_clamp_fusion), kind=kCustom, calls=%fused_computation | custom fusion | bytes 4194432 | tf_op jit(solution)/shard_map/jit(_take)/gather | solution.py:64
  69.8 1.7 fusion.44
  71.5 41.9 %all-to-all-done = bf16[32,32,2,512]{3,1,2,0:T(8,128)(2,1)} async-done(((bf16[32,32,2,512]{3,1,2,0:T(8,128)(2,1)}), bf16[32,32,2,512]{3,1,2,0:T(8,128)(2,1)}, u32[]{:S(2)}, u32[]{:S(2)}) %all-to-all-start) | async-done | bytes 2097184 | tf_op jit(solution)/shard_map/all_to_all | solution.py:43
  113.3 3.0 %fusion.12 = f32[32,32,2,64]{3,1,2,0:T(8,128)S(1)} fusion(bf16[32,32,2,512]{3,1,2,0:T(8,128)(2,1)} %all-to-all-done, bf16[32,512,64]{1,2,0:T(8,128)(2,1)} %gather_fusion, pred[32]{0:T(512)(128)(4,1)S(1)} %get-tuple-element.18), kind=kOutput, calls=%fused_computation.15 | convolution fusion | flops 135266304 | bytes 4718624 | tf_op jit(solution)/shard_map/gjsd,gdr->gjsr/dot_general | solution.py:66
  116.3 1.3 pad_maximum_fusion
  117.7 58.2 %all-reduce.2 = bf16[32,32,2,128]{3,1,2,0:T(8,128)(2,1)S(1)} all-reduce(f32[32,32,2,128]{3,1,2,0:T(8,128)} %pad_maximum_fusion), channel_id=1, replica_groups=mesh['dp'=32,'tensor'=16] {'tensor'}, use_global_device_ids=true, to_apply=%region_6.7 | all-reduce | flops 262144 | bytes 1572864 | tf_op jit(solution)/shard_map/psum | solution.py:68
  175.9 2.2 %fusion.27 = bf16[32,32,2,128]{3,1,2,0:T(8,128)(2,1)} fusion(bf16[32,64,128]{2,1,0:T(8,128)(2,1)} %gather_fusion.1, pred[32]{0:T(512)(128)(4,1)S(1)} %get-tuple-element.18, bf16[32,32,2,128]{3,1,2,0:T(8,128)(2,1)S(1)} %all-reduce.2), kind=kOutput, calls=%fused_computation.26 | convolution fusion | flops 34340864 | bytes 1572896 | tf_op jit(solution)/shard_map/gjsr,grk->gjsk/dot_general | solution.py:72
  178.1 6.0 %all-to-all-start.3 = ((bf16[32,32,2,128]{3,1,2,0:T(8,128)(2,1)}), bf16[32,32,2,128]{3,1,2,0:T(8,128)(2,1)S(1)}, u32[]{:S(2)}, u32[]{:S(2)}) async-start(bf16[32,32,2,128]{3,1,2,0:T(8,128)(2,1)} %fusion.27), calls=%async_computation.4 | async-start | bytes 1048576 | tf_op jit(solution)/shard_map/all_to_all | solution.py:43
  184.3 7.1 %fusion.22 = bf16[16,512,64]{1,2,0:T(8,128)(2,1)} fusion(bf16[32,32,2,512]{3,1,2,0:T(8,128)(2,1)} %all-to-all-done, pred[32,16]{1,0:T(8,128)(4,1)S(1)} %iota_compare_fusion.6, bf16[32,32,2,64]{3,1,2,0:T(8,128)(2,1)S(1)} %get-tuple-element.21), kind=kOutput, calls=%fused_computation.24 | convolution fusion | flops 2150629376 | bytes 3408384 | tf_op jit(solution)/shard_map/gjsd,gjstr->tdr/dot_general | solution.py:76
  191.4 4.9 %fusion.34 = bf16[16,64,128]{2,1,0:T(8,128)(2,1)} fusion(pred[32,16]{1,0:T(8,128)(4,1)S(1)} %iota_compare_fusion.6, bf16[32,32,2,64]{3,1,2,0:T(8,128)(2,1)S(1)} %get-tuple-element.20, bf16[32,32,2,128]{3,1,2,0:T(8,128)(2,1)} %all-to-all-done.2, f32[32,32]{1,0:T(8,128)S(1)} %multiply_subtract_fusion), kind=kOutput, calls=%fused_computation.29 | convolution fusion | flops 540016640 | bytes 1053184 | tf_op jit(solution)/shard_map/gjstr,gjsk->trk/dot_general | solution.py:78
  196.2 1.4 all-to-all-done.3
  197.7 1.3 fusion.37
  199.0 0.8 copy.70
  (45 shorter events, 4.5 us)
Async XLA Ops:
  7.2 1.6 copy-start
  7.2 190.5 %reduce-scatter.2.cloned.1.call-start = ((), (), s32[]{:S(2)}) async-start(), calls=%async_computation.5 | async-start | bytes 4456448 | tf_op jit(solution)/shard_map/reduce_scatter | solution.py:49
  13.0 0.7 copy-start.5
  13.0 1.5 copy-start.7
  13.0 16.1 %copy-start.8 = (bf16[256,2,128]{2,1,0:T(2,128)(2,1)S(1)}, bf16[256,2,128]{2,1,0:T(2,128)(2,1)}, u32[]{:S(2)}) copy-start(bf16[256,2,128]{2,1,0:T(2,128)(2,1)} %param.17) | copy-start | bytes 393220
  13.0 30.4 %copy-start.2 = (bf16[256,2,512]{2,1,0:T(2,128)(2,1)S(1)}, bf16[256,2,512]{2,1,0:T(2,128)(2,1)}, u32[]{:S(2)}) copy-start(bf16[256,2,512]{2,1,0:T(2,128)(2,1)} %param.9) | copy-start | bytes 1572868
  15.7 21.6 %all-to-all-start.1 = ((f32[32,32,2]{1,2,0:T(2,128)}), f32[32,32,2]{1,2,0:T(2,128)S(1)}, u32[]{:S(2)}, u32[]{:S(2)}) async-start(f32[32,32,2]{1,2,0:T(2,128)} %copy.63), calls=%async_computation.2 | async-start | bytes 65536 | tf_op jit(solution)/shard_map/all_to_all | solution.py:43
  37.3 22.0 %all-to-all-start.2 = ((bf16[32,32,2,128]{3,1,2,0:T(8,128)(2,1)}), bf16[32,32,2,128]{3,1,2,0:T(8,128)(2,1)}, u32[]{:S(2)}, u32[]{:S(2)}) async-start(bf16[32,32,2,128]{3,1,2,0:T(8,128)(2,1)} %copy.68), calls=%async_computation.3 | async-start | bytes 1048576 | tf_op jit(solution)/shard_map/all_to_all | solution.py:43
  45.9 19.4 %copy-start.4 = (s32[32,32]{1,0:T(8,128)S(1)}, s32[32,32]{1,0:T(8,128)}, u32[]{:S(2)}) copy-start(s32[32,32]{1,0:T(8,128)} %param.14) | copy-start | bytes 12292
  45.9 19.6 %copy-start.6 = (s32[512]{0:T(512)S(1)}, s32[512]{0:T(512)}, u32[]{:S(2)}) copy-start(s32[512]{0:T(512)} %param.15) | copy-start | bytes 6148
  45.9 19.8 %copy-start.3 = (bf16[16,64,128]{2,1,0:T(8,128)(2,1)S(1)}, bf16[16,64,128]{2,1,0:T(8,128)(2,1)}, u32[]{:S(2)}) copy-start(bf16[16,64,128]{2,1,0:T(8,128)(2,1)} %param.12) | copy-start | bytes 786436
  45.9 21.3 %copy-start.1 = (bf16[16,512,64]{1,2,0:T(8,128)(2,1)S(1)}, bf16[16,512,64]{1,2,0:T(8,128)(2,1)}, u32[]{:S(2)}) copy-start(bf16[16,512,64]{1,2,0:T(8,128)(2,1)} %param.11) | copy-start | bytes 3145732
  59.2 54.1 %all-to-all-start = ((bf16[32,32,2,512]{3,1,2,0:T(8,128)(2,1)}), bf16[32,32,2,512]{3,1,2,0:T(8,128)(2,1)}, u32[]{:S(2)}, u32[]{:S(2)}) async-start(bf16[32,32,2,512]{3,1,2,0:T(8,128)(2,1)} %copy.61), calls=%async_computation.1 | async-start | bytes 4194304 | tf_op jit(solution)/shard_map/all_to_all | solution.py:43
  178.1 19.6 %all-to-all-start.3 = ((bf16[32,32,2,128]{3,1,2,0:T(8,128)(2,1)}), bf16[32,32,2,128]{3,1,2,0:T(8,128)(2,1)S(1)}, u32[]{:S(2)}, u32[]{:S(2)}) async-start(bf16[32,32,2,128]{3,1,2,0:T(8,128)(2,1)} %fusion.27), calls=%async_computation.4 | async-start | bytes 1048576 | tf_op jit(solution)/shard_map/all_to_all | solution.py:43
Sparse Core Ops, SparseCore 0:
  13.1 70.8 reduce-scatter.1

commit v2 on v1

v2 whole, which is shorter than its diff:
```python
import functools

import jax
import jax.numpy as jnp
from jax import lax
from jax.experimental import pallas as pl
from jax.experimental.pallas import tpu as pltpu
from jax.sharding import PartitionSpec as P

adapter_output_scale = 0.25
bf16, f32, i32 = jnp.bfloat16, jnp.float32, jnp.int32
MESH = pl.DeviceIdType.MESH
NT = (((1,), (1,)), ((), ()))


def dot(a, b):
    return jnp.dot(a, b, preferred_element_type=f32)


def dot_nt(a, b):
    return lax.dot_general(a, b, NT, preferred_element_type=f32)


def kernel(
    nz, nx, ny, most, width, kv, rank,
    tau, rows_x, place_row, place_col, marks, same, tau_lane, w_hbm, down_hbm, up_hbm,
    kv_out, gd_out, gu_out,
    w, down, up, sbuf, rbuf, marks_in, adv, wbuf, part, rs_in, ag_out, ag_in,
    dout, din, acc_d, acc_u, base_a, base_b, base_own, base_send, base_in,
    load_sem, rows_s, rows_r, marks_s, marks_r, rs_s, rs_r, ag_s, ag_r, del_s, del_r,
    ba_s, ba_r, by_s, by_r,
):
    groups, tensors = nz * nx, 2 * ny
    att = rows_x.shape[0]
    task_dev = down.shape[0]
    me, mt = lax.axis_index("dp"), lax.axis_index("tensor")
    mz, mx = lax.div(me, nx), lax.rem(me, nx)
    my, core = lax.div(mt, 2), lax.rem(mt, 2)
    sibling = mt + 1 - 2 * core
    own = (nx - 1) * nz
    span = nz * most

    def target(c, dz):
        return lax.rem(mz + dz, nz) * nx + lax.rem(mx + c + 1, nx)

    def origin(c, dz):
        return lax.rem(mz + nz - dz, nz) * nx + lax.rem(mx + 2 * nx - c - 1, nx)

    def remote(src, dst, s, r, dp, tensor):
        return pltpu.make_async_remote_copy(
            src_ref=src, dst_ref=dst, send_sem=s, recv_sem=r,
            device_id=(dp, tensor), device_id_type=MESH,
        )

    loads = [
        pltpu.make_async_copy(src, dst, load_sem.at[i])
        for i, (src, dst) in enumerate(((w_hbm, w), (down_hbm, down), (up_hbm, up)))
    ]
    for load in loads:
        load.start()

    barrier = pltpu.get_barrier_semaphore()

    def greet_groups(i, _):
        other = lax.rem(me + i, groups)
        pl.semaphore_signal(barrier, inc=1, device_id=(other, mt), device_id_type=MESH)
        return 0

    def greet_tensors(i, _):
        other = lax.rem(mt + i, tensors)
        pl.semaphore_signal(barrier, inc=1, device_id=(me, other), device_id_type=MESH)
        return 0

    lax.fori_loop(1, groups, greet_groups, 0)
    lax.fori_loop(1, tensors, greet_tensors, 0)

    def bucket(c):
        places = lax.broadcasted_iota(i32, (span, att), 0) + c * span
        hot = jnp.where(places == place_row[...], 1.0, 0.0).astype(bf16)
        out = dot(hot, rows_x[...]).astype(bf16).reshape(nz, most, rows_x.shape[1])
        sbuf[c * nz : (c + 1) * nz] = out
        if c == nx - 1:
            rbuf[own] = out[0]

    def send_rows(c):
        for dz in sorted(range(nz), key=lambda d: -min(d, nz - d)):
            k = c * nz + dz
            if k != own:
                remote(sbuf.at[k], rbuf.at[k], rows_s, rows_r.at[k], target(c, dz), mt).start()

    bucket(0)
    pl.semaphore_wait(barrier, groups - 1 + tensors - 1)
    for c in range(nx):
        for dz in range(nz):
            k = c * nz + dz
            if k != own:
                remote(marks.at[k], marks_in.at[k], marks_s, marks_r, target(c, dz), mt).start()
    marks_in[own] = marks[own]
    send_rows(0)
    for c in range(1, nx):
        bucket(c)
        send_rows(c)

    loads[0].wait()

    def other_blocks(b, _):
        cols = pl.ds(pl.multiple_of((2 * b + 1 - core) * kv, kv), kv)
        block = w[:, cols]
        for s in range(2):
            base_a[b, :, s * kv : (s + 1) * kv] = dot(
                rows_x[:, s * width : (s + 1) * width], block
            ).astype(bf16)
        return 0

    lax.fori_loop(0, ny, other_blocks, 0)
    exchange = remote(base_a, base_b, ba_s, ba_r, me, sibling)
    exchange.start()

    def own_blocks(b, _):
        cols = pl.ds(pl.multiple_of((2 * b + core) * kv, kv), kv)
        block = w[:, cols]
        for s in range(2):
            base_own[b, :, s * kv : (s + 1) * kv] = dot(
                rows_x[:, s * width : (s + 1) * width], block
            )
        return 0

    lax.fori_loop(0, ny, own_blocks, 0)
    acc_d[...] = jnp.zeros_like(acc_d)
    acc_u[...] = jnp.zeros_like(acc_u)
    exchange.wait_recv()

    def spread_base(i, _):
        y = lax.rem(my + i, ny)
        base_send[y] = (base_own[y] + base_b[y].astype(f32)).astype(bf16)
        remote(base_send.at[y], base_in.at[i], by_s, by_r, me, 2 * y + core).start()
        return 0

    lax.fori_loop(1, ny, spread_base, 0)

    remote(
        marks.at[pl.ds(0, groups - 1)], marks_in.at[pl.ds(0, groups - 1)], marks_s, marks_r, me, sibling
    ).wait_recv()
    mark = marks_in[:, 0, :]
    lane = lax.broadcasted_iota(i32, mark.shape, 1)
    row = lax.broadcasted_iota(i32, mark.shape, 0)
    sums = jnp.sum(jnp.where(lane < most, mark, 0.0), axis=1, keepdims=True)
    counts = jnp.sum(jnp.where(lane >= 64, mark, 0.0), axis=1, keepdims=True)
    sums = jnp.sum(same[...] * sums, axis=0, keepdims=True)
    counts = jnp.sum(same[...] * counts, axis=0, keepdims=True)
    mean = sums / jnp.maximum(counts, 1.0)
    mean = jnp.sum(jnp.where(lane == row, mean, 0.0), axis=1, keepdims=True)
    centred = mark - mean
    diagonal = lax.broadcasted_iota(i32, (most, 128), 0) == lax.broadcasted_iota(i32, (most, 128), 1)
    for k in range(groups):
        column = jnp.sum(jnp.where(diagonal, centred[k : k + 1], 0.0), axis=1, keepdims=True)
        adv[k] = jnp.broadcast_to(column, (most, 128))
    loads[1].wait()
    loads[2].wait()

    def chunk(c, _):
        for dz in range(nz):
            k = c * nz + dz

            def arrive(k=k, dz=dz):
                remote(
                    sbuf.at[k], rbuf.at[k], rows_s, rows_r.at[k], origin(c, dz), mt
                ).wait_recv()

            if dz == 0:
                pl.when(c != nx - 1)(arrive)
            else:
                arrive()
            task = tau[k]
            for s in range(2):
                cot = rbuf[k, :, 2 * width + s * kv : 2 * width + (s + 1) * kv].astype(f32)
                wbuf[c, s, dz] = (adv[k][:, :kv] * cot).astype(bf16)
            both = jnp.concatenate([rbuf[k, :, :width], rbuf[k, :, width : 2 * width]], axis=0)
            heavy = jnp.concatenate([wbuf[c, 0, dz], wbuf[c, 1, dz]], axis=0)
            inner = jnp.concatenate([dot_nt(both, down[task]), dot_nt(heavy, up[task])], axis=1)
            part[c, dz] = inner[:most]
            part[c, nz + dz] = inner[most:]

        def scatter(i, _):
            to = lax.rem(mt + i, tensors)
            remote(part.at[c, to], rs_in.at[c, i - 1], rs_s, rs_r.at[c], me, to).start()
            return 0

        lax.fori_loop(1, tensors, scatter, 0)
        remote(
            part.at[c, pl.ds(0, tensors - 1)], rs_in.at[c], rs_s, rs_r.at[c], me, sibling
        ).wait_recv()
        total = part[c, mt]
        for i in range(tensors - 1):
            total = total + rs_in[c, i]
        ag_out[c] = total.astype(bf16)
        ag_in[c, mt] = total.astype(bf16)

        def gather(i, _):
            to = lax.rem(mt + i, tensors)
            remote(ag_out.at[c], ag_in.at[c, mt], ag_s, ag_r.at[c], me, to).start()
            return 0

        lax.fori_loop(1, tensors, gather, 0)
        remote(
            ag_in.at[c, pl.ds(0, tensors - 1)], ag_in.at[c, pl.ds(0, tensors - 1)], ag_s,
            ag_r.at[c], me, sibling,
        ).wait_recv()

        for dz in range(nz):
            k = c * nz + dz
            task = tau[k]
            inner = jnp.concatenate([ag_in[c, dz], ag_in[c, nz + dz]], axis=0)[:, :rank]
            delta = (adapter_output_scale * dot(inner, up[task])).astype(bf16)
            delta = jnp.concatenate([delta[:most], delta[most:]], axis=1)
            dout[k] = delta

            def give_back(k=k, dz=dz):
                remote(dout.at[k], din.at[k], del_s, del_r, origin(c, dz), mt).start()

            if dz == 0:
                pl.when(c != nx - 1)(give_back)
            else:
                give_back()

        inner = ag_in[c].reshape(tensors * most, 2 * rank).astype(f32).T
        inner_d, inner_b = inner[:rank].astype(bf16), inner[rank:].astype(bf16)
        task_lane = tau_lane[c]
        some = task_dev // acc_d.shape[0]
        weighted = wbuf[c].reshape(2 * span, kv)

        def gradients(q, _):
            hots = [
                jnp.where(task_lane == q * some + i, 1.0, 0.0).astype(bf16) for i in range(some)
            ]
            spread = jnp.concatenate([inner_b * hot for hot in hots], axis=0)
            terms = acc_d[q]
            for s in range(2):
                rows = rbuf[pl.ds(c * nz, nz), :, s * width : (s + 1) * width]
                terms = terms + dot(
                    spread[:, s * span : (s + 1) * span], rows.reshape(span, width)
                )
            acc_d[q] = terms
            spread = jnp.concatenate([inner_d * hot for hot in hots], axis=0)
            acc_u[q] += dot(spread, weighted)
            return 0

        lax.fori_loop(0, acc_d.shape[0], gradients, 0)
        return 0

    lax.fori_loop(0, nx, chunk, 0)

    some = task_dev // acc_d.shape[0]
    for q in range(acc_d.shape[0]):
        gd_out[q * some : (q + 1) * some] = (
            (adapter_output_scale * acc_d[q]).astype(bf16).reshape(some, rank, width)
        )
        gu_out[q * some : (q + 1) * some] = (
            (adapter_output_scale * acc_u[q]).astype(bf16).reshape(some, rank, kv)
        )
    remote(
        base_send.at[pl.ds(0, ny - 1)], base_in.at[pl.ds(1, ny - 1)], by_s, by_r, me, sibling
    ).wait_recv()
    total = base_own[my] + base_b[my].astype(f32)
    for i in range(1, ny):
        total = total + base_in[i].astype(f32)
    din[own] = dout[own]
    remote(
        dout.at[pl.ds(0, groups - 1)], din.at[pl.ds(0, groups - 1)], del_s, del_r, me, sibling
    ).wait_recv()
    places = lax.broadcasted_iota(i32, (att, groups * most), 1)
    hot = jnp.where(places == place_col[...], 1.0, 0.0).astype(bf16)
    delta = dot(hot, din[...].reshape(groups * most, 2 * kv))
    kv_out[...] = (total + delta).astype(bf16)

    remote(
        sbuf.at[pl.ds(0, groups - 1)], rbuf.at[pl.ds(0, groups - 1)], rows_s, rows_r.at[0], me, sibling
    ).wait_send()
    remote(
        marks.at[pl.ds(0, groups - 1)], marks_in.at[pl.ds(0, groups - 1)], marks_s, marks_r, me, sibling
    ).wait_send()
    exchange.wait_send()
    remote(
        base_send.at[pl.ds(0, ny - 1)], base_in.at[pl.ds(1, ny - 1)], by_s, by_r, me, sibling
    ).wait_send()
    remote(
        rs_in, rs_in, rs_s, rs_r.at[0], me, sibling
    ).wait_send()
    remote(
        ag_in.at[:, pl.ds(0, tensors - 1)], ag_in.at[:, pl.ds(0, tensors - 1)], ag_s, ag_r.at[0],
        me, sibling,
    ).wait_send()
    remote(
        dout.at[pl.ds(0, groups - 1)], din.at[pl.ds(0, groups - 1)], del_s, del_r, me, sibling
    ).wait_send()


def body(
    nz,
    most,
    hidden,
    key_value_weight,
    adapter_down_weight,
    adapter_up_weight,
    attempt_adapter_slot,
    group_slot_task,
    task_row_position,
    scores,
    cotangent,
):
    groups, tensors = lax.axis_size("dp"), lax.axis_size("tensor")
    nx, ny = groups // nz, tensors // 2
    me = lax.axis_index("dp")
    att, steps, width = hidden.shape
    task_dev, _, rank = adapter_down_weight.shape
    kv = cotangent.shape[2]
    slot = attempt_adapter_slot[:, 0]
    mz, mx = me // nx, me % nx
    off_z, off_x = (slot // nx - mz) % nz, (slot % nx - mx - 1) % nx
    order = jnp.arange(att, dtype=i32)
    earlier = (order[:, None] > order[None, :]) & (slot[:, None] == slot[None, :])
    place = (off_x * nz + off_z) * most + jnp.sum(earlier.astype(i32), axis=1)
    here = jnp.arange(groups * most, dtype=i32)[:, None] == place[None, :]
    score_at = jnp.sum(jnp.where(here, scores[None, :], 0), axis=1).reshape(groups, most)
    count_at = jnp.sum(here.astype(i32), axis=1).reshape(groups, most)
    marks = jnp.concatenate(
        [
            jnp.pad(score_at, ((0, 0), (0, 64 - most))),
            jnp.pad(count_at, ((0, 0), (0, 64 - most))),
        ],
        axis=1,
    ).astype(f32)[:, None, :]
    ks = jnp.arange(groups, dtype=i32)
    from_group = ((mz - ks % nz) % nz) * nx + (mx - ks // nz - 1) % nx
    my_tasks = lax.dynamic_index_in_dim(group_slot_task, me, 1, keepdims=False)
    ids = jnp.arange(groups, dtype=i32)
    task_of = jnp.sum(jnp.where(from_group[:, None] == ids[None, :], my_tasks[None, :], 0), axis=1)
    task_ids = jnp.arange(task_row_position.shape[0], dtype=i32)
    stored = jnp.sum(
        jnp.where(task_of[:, None] == task_ids[None, :], task_row_position[None, :], 0), axis=1
    )
    tau = stored % task_dev
    same = (tau[:, None] == tau[None, :]).astype(f32)
    same = jnp.pad(same, ((0, 0), (0, 128 - groups)))
    tau_lane = jnp.broadcast_to(tau.reshape(nx, 1, 1, nz, 1), (nx, 1, 2, nz, most))
    tau_lane = tau_lane.reshape(nx, 1, 2 * nz * most)
    rows_x = jnp.concatenate(
        [hidden.reshape(att, 2 * width), cotangent.reshape(att, 2 * kv)], axis=1
    )
    wide = 2 * width + 2 * kv
    vmem, dma = pltpu.VMEM, pltpu.SemaphoreType.DMA
    in_vmem = pl.BlockSpec(memory_space=pltpu.VMEM)
    anywhere = pl.BlockSpec(memory_space=pl.ANY)
    quads = task_dev // 4
    kv_new, grad_down, grad_up = pl.pallas_call(
        functools.partial(kernel, nz, nx, ny, most, width, kv, rank),
        out_shape=(
            jax.ShapeDtypeStruct((att, 2 * kv), bf16),
            jax.ShapeDtypeStruct((task_dev, rank, width), bf16),
            jax.ShapeDtypeStruct((task_dev, rank, kv), bf16),
        ),
        in_specs=[pl.BlockSpec(memory_space=pltpu.SMEM)] + [in_vmem] * 6 + [anywhere] * 3,
        out_specs=(in_vmem, in_vmem, in_vmem),
        scratch_shapes=[
            vmem(key_value_weight.shape, bf16),
            vmem((task_dev, rank, width), bf16),
            vmem((task_dev, rank, kv), bf16),
            vmem((groups, most, wide), bf16),
            vmem((groups, most, wide), bf16),
            vmem((groups, 1, 128), f32),
            vmem((groups, most, 128), f32),
            vmem((nx, 2, nz, most, kv), bf16),
            vmem((nx, tensors, most, 2 * rank), f32),
            vmem((nx, tensors - 1, most, 2 * rank), f32),
            vmem((nx, most, 2 * rank), bf16),
            vmem((nx, tensors, most, 2 * rank), bf16),
            vmem((groups, most, 2 * kv), bf16),
            vmem((groups, most, 2 * kv), bf16),
            vmem((quads, 4 * rank, width), f32),
            vmem((quads, 4 * rank, kv), f32),
            vmem((ny, att, 2 * kv), bf16),
            vmem((ny, att, 2 * kv), bf16),
            vmem((ny, att, 2 * kv), f32),
            vmem((ny, att, 2 * kv), bf16),
            vmem((ny, att, 2 * kv), bf16),
            dma((3,)),
            dma, dma((groups,)),
            dma, dma,
            dma, dma((nx,)),
            dma, dma((nx,)),
            dma, dma,
            dma, dma,
            dma, dma,
        ],
        compiler_params=pltpu.CompilerParams(
            collective_id=0, has_side_effects=True, vmem_limit_bytes=52 << 20
        ),
    )(
        tau, rows_x, place[None, :], place[:, None], marks, same, tau_lane,
        key_value_weight, jnp.swapaxes(adapter_down_weight, 1, 2), adapter_up_weight,
    )
    return kv_new.reshape(att, steps, kv), jnp.swapaxes(grad_down, 1, 2), grad_up


def solution(mesh):
    in_specs = (
        P("dp", None, "tensor"),
        P("tensor", None),
        P("dp", "tensor", None),
        P("dp", None, "tensor"),
        P("dp", None),
        P(),
        P(),
        P("dp"),
        P("dp", None, "tensor"),
    )
    out_specs = (P("dp", None, "tensor"), P("dp", "tensor", None), P("dp", None, "tensor"))
    return jax.shard_map(
        functools.partial(body, 8, 32),
        mesh=mesh, in_specs=in_specs, out_specs=out_specs, check_vma=False,
    )
```

time: 210 us -> 143 us (0.68); the launches traced: 207 us -> 142 us
  Pallas kernels: 0 us -> 128 us
  waiting for transfers between devices: 63.4 us -> 0 us
  blocking collectives: 58.2 us -> 0 us
  starting transfers between devices: 31.6 us -> 0 us
  matrix products: 25.7 us -> 0 us
  between operations: 14.3 us -> 0.77 us
  local copies, waits for them, and re-layouts: 10.7 us -> 7.61 us
  other arithmetic: 2.78 us -> 5.69 us
    pallas_call x0 -> x1, Pallas kernels: none -> 128 us  [body(): pl.pallas_call(functools.partial(kernel, nz, nx, ny, most, width, kv, ran...]
    all_to_all x4 -> x0, waiting for transfers between devices: 63.4 us -> none  [swap(): return lax.all_to_all(x, 'dp', split_axis=0, concat_axis=0, tiled=True)]
    psum x1 -> x0, blocking collectives: 58.2 us -> none  [body(): lax.psum(jnp.concatenate([inner_down, inner_back], axis=3), 'tensor')]
    all_to_all x4 -> x0, starting transfers between devices: 31.5 us -> none  [swap(): return lax.all_to_all(x, 'dp', split_axis=0, concat_axis=0, tiled=True)]
    dot_general x9 -> x0, matrix products: 25.7 us -> none  [the longest x1 7.05 us: body(): jnp.einsum('gjsd,gjstr->tdr', hid, spread, preferred_element_type=f32)]
    gather x2 -> x0, local copies, waits for them, and re-layouts: 3.5 us -> none  [the longest x1 2.07 us: body(): down = jnp.take(adapter_down_weight, local, axis=0)]
    unnamed x20 -> x11, local copies, waits for them, and re-layouts: 3.08 us -> 6.03 us
  transfers between devices with their start and end apart: 5 -> 0, of which waited for: 4 -> 0; matrix products, arithmetic and copies ran while one was open for 15% -> 0% of each run, Pallas kernels for 0% -> 0%
where the time goes in v2:
time: 143 us; the launch traced here: 142 us
  Pallas kernels  128 us (90%)
  local copies, waits for them, and re-layouts  7.61 us (5%)
  other arithmetic  5.69 us (4%)
    pallas_call x1, Pallas kernels, body(): pl.pallas_call(functools.partial(kernel, nz, nx, ny, most, width, kv, ran...  128 us
    unnamed x11, local copies, waits for them, and re-layouts  6.03 us

profile of v2, /device:TPU:6, one launch (start us, length us, event | category | flops | bytes accessed | tf_op | source)
XLA Modules:
  0.0 141.8 jit_solution(2038041863604862428)
XLA Ops:
  0.7 0.7 copy-done
  1.4 0.2 dynamic-slice_reduce_fusion
  1.6 0.2 select_reduce_fusion.2
  1.7 0.9 select_reduce_fusion.1
  2.6 0.9 convert_reduce_fusion.1
  3.6 0.7 multiply_add_fusion.1.place_row
  4.3 0.7 multiply_add_fusion
  5.0 0.7 broadcast_compare_fusion.1
  5.7 0.1 reduce_sum.58
  5.8 0.1 broadcast_compare_fusion
  5.8 1.1 select_reduce_fusion
  7.1 0.1 add_convert_fusion.marks
  7.2 0.1 broadcast_in_dim.68
  7.3 0.1 broadcast_in_dim.69.tau_lane
  7.3 0.2 copy.31
  7.5 0.1 copy.34
  7.7 0.9 copy.49
  8.6 0.8 copy.28
  9.4 0.3 fusion.7.place_col
  9.8 0.6 copy-done.1
  10.4 127.7 %shard_map.112 = (bf16[256,256]{1,0:T(8,128)(2,1)S(1)}, bf16[16,64,512]{2,1,0:T(8,128)(2,1)}, bf16[16,64,128]{2,1,0:T(8,128)(2,1)S(1)}) custom-call(s32[32]{0:T(128)S(1)} %and_select_fusion.8.tau, bf16[256,1280]{1,0:T(8,128)(2,1)S(1)} %pad_maximum_fusion.rows_x, s32[1,256]{1,0:T(1,128)S(1)} %multiply_add_fusion.1.place_row, s32[256,1]{1,0:T(8,128)S(1)} %fusion.7.place_col, ...), custom_call_target="tpu_custom_call" | custom-call | tf_op jit(solution)/shard_map/pallas_call | solution.py:355
  138.1 0.7 reshape.355
  138.8 2.3 %copy.52 = bf16[16,512,64]{1,2,0:T(8,128)(2,1)} copy(bf16[16,512,64]{1,2,0:T(8,128)(2,1)} %bitcast.30) | data formatting | bytes 2097152
  141.1 0.7 copy.53
  (14 shorter events, 0.3 us)
Async XLA Ops:
  0.6 0.7 copy-start
  0.6 9.1 %copy-start.2 = (bf16[256,2,512]{2,1,0:T(2,128)(2,1)S(1)}, bf16[256,2,512]{2,1,0:T(2,128)(2,1)}, u32[]{:S(2)}) copy-start(bf16[256,2,512]{2,1,0:T(2,128)(2,1)} %param.9) | copy-start | bytes 1572868
  9.4 1.0 copy-start.1

commit v3 on v1

v3 whole, which is shorter than its diff:
```python
import functools

import jax
import jax.numpy as jnp
from jax import lax
from jax.experimental import pallas as pl
from jax.experimental.pallas import tpu as pltpu
from jax.sharding import PartitionSpec as P

adapter_output_scale = 0.25
bf16, f32, i32 = jnp.bfloat16, jnp.float32, jnp.int32
MESH = pl.DeviceIdType.MESH
NT = (((1,), (1,)), ((), ()))
COUNTS_FROM = 64


def dot(a, b):
    return jnp.dot(a, b, preferred_element_type=f32)


def dot_nt(a, b):
    return lax.dot_general(a, b, NT, preferred_element_type=f32)


def iota(shape, axis):
    return lax.broadcasted_iota(i32, shape, axis)


def kernel(
    nz, nx, ny, most, width, kv, rank,
    slot_task, task_row, slot, scores, rows_x, w_hbm, down_hbm, up_hbm,
    kv_out, acc_d, acc_u,
    tau, w, down, up, sbuf, rbuf, marks, marks_in, places, adv, tau_lane, wbuf, part, pair_in, pair,
    rs_in, ag_out, ag_in, dout, din, base_a, base_b, base_own, base_send, base_in,
    load_sem, rows_s, rows_r, marks_s, marks_r, pair_s, pair_r, rs_s, rs_r, ag_s, ag_r,
    del_s, del_r, ba_s, ba_r, by_s, by_r,
):
    groups, tensors, half = nz * nx, 2 * ny, nz // 2
    att = rows_x.shape[0]
    task_dev = down.shape[0]
    some = task_dev // acc_d.shape[0]
    me, mt = lax.axis_index("dp"), lax.axis_index("tensor")
    mz, mx = lax.div(me, nx), lax.rem(me, nx)
    my, core = lax.div(mt, 2), lax.rem(mt, 2)
    sibling = mt + 1 - 2 * core
    own = (nx - 1) * nz
    span = nz * most

    def target(c, u):
        return lax.rem(mz + u, nz) * nx + lax.rem(mx + c + 1, nx)

    def origin(c, u):
        return lax.rem(mz + nz - u, nz) * nx + lax.rem(mx + 2 * nx - c - 1, nx)

    def remote(src, dst, s, r, dp, tensor):
        return pltpu.make_async_remote_copy(
            src_ref=src, dst_ref=dst, send_sem=s, recv_sem=r,
            device_id=(dp, tensor), device_id_type=MESH,
        )

    def peers(ref, count):
        return ref.at[pl.ds(0, count)]

    barrier = pltpu.get_barrier_semaphore()

    def greet_groups(i, _):
        other = lax.rem(me + i, groups)
        pl.semaphore_signal(barrier, inc=1, device_id=(other, mt), device_id_type=MESH)
        return 0

    def greet_tensors(i, _):
        other = lax.rem(mt + i, tensors)
        pl.semaphore_signal(barrier, inc=1, device_id=(me, other), device_id_type=MESH)
        return 0

    lax.fori_loop(1, groups, greet_groups, 0)
    lax.fori_loop(1, tensors, greet_tensors, 0)
    loads = [
        pltpu.make_async_copy(src, dst, load_sem.at[i])
        for i, (src, dst) in enumerate(((w_hbm, w), (down_hbm, down), (up_hbm, up)))
    ]
    for load in loads:
        load.start()

    square = (att, att)
    diagonal = iota(square, 0) == iota(square, 1)
    slot_row = slot[...]
    slot_col = jnp.sum(jnp.where(diagonal, slot_row.astype(f32), 0.0), axis=1, keepdims=True)
    earlier = (iota(square, 0) < iota(square, 1)) & (slot_col == slot_row.astype(f32))
    rank_row = jnp.sum(jnp.where(earlier, 1.0, 0.0), axis=0, keepdims=True)
    off_z = lax.rem(lax.div(slot_row, nx) + nz - mz, nz)
    off_x = lax.rem(lax.rem(slot_row, nx) + 2 * nx - mx - 1, nx)
    k_row = off_x * nz + off_z
    place_row = (k_row * most).astype(f32) + rank_row
    place_col = jnp.sum(jnp.where(diagonal, place_row, 0.0), axis=1, keepdims=True).astype(i32)
    place_row = place_row.astype(i32)
    places[...] = jnp.broadcast_to(place_col, (att, 128))

    def bucket(c):
        hot = jnp.where(iota((span, att), 0) + c * span == place_row, 1.0, 0.0).astype(bf16)
        out = dot(hot, rows_x[...]).astype(bf16).reshape(nz, most, rows_x.shape[1])
        sbuf[c * nz : (c + 1) * nz] = out
        if c == nx - 1:
            rbuf[own] = out[0]

    def send_rows(c):
        for u in sorted(range(nz), key=lambda d: -min(d, nz - d)):
            k = c * nz + u
            if k != own:
                remote(sbuf.at[k], rbuf.at[k], rows_s, rows_r.at[k], target(c, u), mt).start()

    def make_marks():
        k_hot = k_row == iota((groups, att), 0)
        ranks = lax.rem(place_col, most)
        lanes = iota((att, 128), 1)
        to_score = jnp.where(ranks == lanes, 1.0, 0.0).astype(bf16)
        to_count = jnp.where(ranks + COUNTS_FROM == lanes, 1.0, 0.0).astype(bf16)
        score = jnp.where(k_hot, scores[...].astype(f32), 0.0).astype(bf16)
        count = jnp.where(k_hot, 1.0, 0.0).astype(bf16)
        mark = dot(score, to_score) + dot(count, to_count)
        for k in range(groups):
            marks[k] = mark[k : k + 1]
        marks_in[own] = marks[own]

    def send_marks():
        for c in range(nx):
            for u in range(nz):
                k = c * nz + u
                if k != own:
                    remote(marks.at[k], marks_in.at[k], marks_s, marks_r, target(c, u), mt).start()

    def find_tasks():
        lane, row = iota((groups, 128), 1), iota((groups, 128), 0)
        by_row, by_lane = jnp.full((groups, 128), -1, i32), jnp.full((groups, 128), -2, i32)
        for k in range(groups):
            task = lax.rem(task_row[slot_task[origin(k // nz, k % nz), me]], task_dev)
            tau[k] = task
            by_row = jnp.where(row == k, task, by_row)
            by_lane = jnp.where(lane == k, task, by_lane)
        lane = iota((1, 2 * span), 1)
        place = lax.div(lane, span) * half + lax.rem(lax.div(lane, most), half)
        for c in range(nx):
            line = jnp.zeros((1, 2 * span), i32)
            for u in range(nz):
                line = jnp.where(place == u, tau[c * nz + u], line)
            tau_lane[c] = line
        return jnp.where(by_row == by_lane, 1.0, 0.0)

    def advantages(same):
        remote(
            peers(marks, groups - 1), peers(marks_in, groups - 1), marks_s, marks_r, me, sibling
        ).wait_recv()
        mark = marks_in[:, 0, :]
        lane, row = iota(mark.shape, 1), iota(mark.shape, 0)
        sums = jnp.sum(jnp.where(lane < most, mark, 0.0), axis=1, keepdims=True)
        counts = jnp.sum(jnp.where(lane >= COUNTS_FROM, mark, 0.0), axis=1, keepdims=True)
        sums = jnp.sum(same * sums, axis=0, keepdims=True)
        counts = jnp.sum(same * counts, axis=0, keepdims=True)
        mean = sums / jnp.maximum(counts, 1.0)
        mean = jnp.sum(jnp.where(lane == row, mean, 0.0), axis=1, keepdims=True)
        centred = mark - mean
        corner = iota((most, 128), 0) == iota((most, 128), 1)
        for k in range(groups):
            column = jnp.sum(jnp.where(corner, centred[k : k + 1], 0.0), axis=1, keepdims=True)
            adv[k] = jnp.broadcast_to(column, (most, 128))

    exchange = remote(base_a, base_b, ba_s, ba_r, me, sibling)

    def other_blocks(b, _):
        cols = pl.ds(pl.multiple_of((2 * b + 1 - core) * kv, kv), kv)
        block = w[:, cols]
        for s in range(2):
            base_a[b, :, s * kv : (s + 1) * kv] = dot(
                rows_x[:, s * width : (s + 1) * width], block
            ).astype(bf16)
        return 0

    def own_blocks(b, _):
        cols = pl.ds(pl.multiple_of((2 * b + core) * kv, kv), kv)
        block = w[:, cols]
        for s in range(2):
            base_own[b, :, s * kv : (s + 1) * kv] = dot(
                rows_x[:, s * width : (s + 1) * width], block
            )
        return 0

    def spread_base(steps):
        for i in steps:
            y = lax.rem(my + i, ny)
            base_send[y] = (base_own[y] + base_b[y].astype(f32)).astype(bf16)
            remote(base_send.at[y], base_in.at[i], by_s, by_r, me, 2 * y + core).start()

    def inner_parts(c):
        for u in range(nz):
            k, h, q = c * nz + u, u // half, u % half
            if k != own:
                remote(sbuf.at[k], rbuf.at[k], rows_s, rows_r.at[k], origin(c, u), mt).wait_recv()
            task = tau[k]
            for s in range(2):
                cot = rbuf[k, :, 2 * width + s * kv : 2 * width + (s + 1) * kv].astype(f32)
                wbuf[c, h, s, q] = (adv[k][:, :kv] * cot).astype(bf16)
            both = jnp.concatenate([rbuf[k, :, :width], rbuf[k, :, width : 2 * width]], axis=0)
            heavy = jnp.concatenate([wbuf[c, h, 0, q], wbuf[c, h, 1, q]], axis=0)
            inner = jnp.concatenate([dot_nt(both, down[task]), dot_nt(heavy, up[task])], axis=1)
            part[c, h, q] = inner[:most]
            part[c, h, half + q] = inner[most:]

    def pair_copy(c):
        return remote(part.at[c, 1 - core], pair_in.at[c], pair_s, pair_r.at[c], me, sibling)

    def scatter(c):
        pair_copy(c).wait_recv()
        pair[c] = part[c, core] + pair_in[c]

        def one(i, _):
            y = lax.rem(my + i, ny)
            remote(
                pair.at[c, y], rs_in.at[c, i - 1], rs_s, rs_r.at[c], me, 2 * y + core
            ).start()
            return 0

        lax.fori_loop(1, ny, one, 0)

    def gather(c):
        remote(
            peers(pair.at[c], ny - 1), rs_in.at[c], rs_s, rs_r.at[c], me, sibling
        ).wait_recv()
        total = pair[c, my]
        for i in range(ny - 1):
            total = total + rs_in[c, i]
        piece = core * ny + my
        ag_out[c] = total.astype(bf16)
        ag_in[c, piece] = total.astype(bf16)

        def one(i, _):
            to = lax.rem(mt + i, tensors)
            remote(ag_out.at[c], ag_in.at[c, piece], ag_s, ag_r.at[c], me, to).start()
            return 0

        lax.fori_loop(1, tensors, one, 0)

    def deltas(c):
        remote(
            peers(ag_in.at[c], tensors - 1), peers(ag_in.at[c], tensors - 1), ag_s, ag_r.at[c],
            me, sibling,
        ).wait_recv()
        for u in range(nz):
            k, h, q = c * nz + u, u // half, u % half
            inner = jnp.concatenate([ag_in[c, h * ny + q], ag_in[c, h * ny + half + q]], axis=0)
            delta = (adapter_output_scale * dot(inner[:, :rank], up[tau[k]])).astype(bf16)
            delta = jnp.concatenate([delta[:most], delta[most:]], axis=1)
            if k == own:
                din[k] = delta
            else:
                dout[k] = delta
                remote(dout.at[k], din.at[k], del_s, del_r, origin(c, u), mt).start()

    def gradients(c):
        inner = ag_in[c].reshape(tensors * most, 2 * rank).astype(f32).T
        inner_d, inner_b = inner[:rank].astype(bf16), inner[rank:].astype(bf16)
        task_lane = tau_lane[c]
        weighted = wbuf[c].reshape(2 * span, kv)

        def one(g, _):
            hots = [
                jnp.where(task_lane == g * some + i, 1.0, 0.0).astype(bf16) for i in range(some)
            ]
            spread = jnp.concatenate([inner_b * hot for hot in hots], axis=0)
            terms = acc_d[g]
            for h in range(2):
                rows = jnp.concatenate(
                    [
                        rbuf[
                            c * nz + h * half : c * nz + (h + 1) * half,
                            :,
                            s * width : (s + 1) * width,
                        ].reshape(half * most, width)
                        for s in range(2)
                    ],
                    axis=0,
                )
                terms = terms + dot(spread[:, h * span : (h + 1) * span], rows)
            acc_d[g] = terms
            spread = jnp.concatenate([inner_d * hot for hot in hots], axis=0)
            acc_u[g] += dot(spread, weighted)
            return 0

        lax.fori_loop(0, acc_d.shape[0], one, 0)

    bucket(0)
    make_marks()
    pl.semaphore_wait(barrier, groups - 1 + tensors - 1)
    send_marks()
    send_rows(0)
    for c in range(1, nx):
        bucket(c)
        send_rows(c)
    loads[0].wait()
    lax.fori_loop(0, ny, other_blocks, 0)
    exchange.start()
    same = find_tasks()
    lax.fori_loop(0, ny, own_blocks, 0)
    acc_d[...] = jnp.zeros_like(acc_d)
    acc_u[...] = jnp.zeros_like(acc_u)
    exchange.wait_recv()
    base_steps = [[3, 5, 1, 7], [2, 6], [4]] if ny == 8 else [list(range(1, ny))]
    spread_base(base_steps[0])
    advantages(same)
    loads[1].wait()
    loads[2].wait()
    for c in range(nx):
        inner_parts(c)
        pair_copy(c).start()
        scatter(c)
        if c > 0:
            gradients(c - 1)
        gather(c)
        if c + 1 < len(base_steps):
            spread_base(base_steps[c + 1])
        deltas(c)
    gradients(nx - 1)

    base_wait = remote(
        peers(base_send, ny - 1), peers(base_in, ny - 1), by_s, by_r, me, sibling
    )
    base_wait.wait_recv()
    total = base_own[my] + base_b[my].astype(f32)
    for i in range(1, ny):
        total = total + base_in[i].astype(f32)
    delta_wait = remote(
        peers(dout, groups - 1), peers(din, groups - 1), del_s, del_r, me, sibling
    )
    delta_wait.wait_recv()
    place = jnp.concatenate([places[...]] * (groups * most // 128), axis=1)
    hot = jnp.where(iota((att, groups * most), 1) == place, 1.0, 0.0).astype(bf16)
    kv_out[...] = (total + dot(hot, din[...].reshape(groups * most, 2 * kv))).astype(bf16)

    remote(
        peers(sbuf, groups - 1), peers(rbuf, groups - 1), rows_s, rows_r.at[0], me, sibling
    ).wait_send()
    remote(
        peers(marks, groups - 1), peers(marks_in, groups - 1), marks_s, marks_r, me, sibling
    ).wait_send()
    exchange.wait_send()
    base_wait.wait_send()
    delta_wait.wait_send()
    remote(pair_in, pair_in, pair_s, pair_r.at[0], me, sibling).wait_send()
    remote(rs_in, rs_in, rs_s, rs_r.at[0], me, sibling).wait_send()
    sent = ag_in.at[:, pl.ds(0, tensors - 1)]
    remote(sent, sent, ag_s, ag_r.at[0], me, sibling).wait_send()


def body(
    nz,
    most,
    hidden,
    key_value_weight,
    adapter_down_weight,
    adapter_up_weight,
    attempt_adapter_slot,
    group_slot_task,
    task_row_position,
    scores,
    cotangent,
):
    groups, tensors = lax.axis_size("dp"), lax.axis_size("tensor")
    nx, ny = groups // nz, tensors // 2
    att, steps, width = hidden.shape
    task_dev, _, rank = adapter_down_weight.shape
    kv = cotangent.shape[2]
    rows_x = jnp.concatenate(
        [hidden.reshape(att, 2 * width), cotangent.reshape(att, 2 * kv)], axis=1
    )
    wide = 2 * width + 2 * kv
    vmem, dma = pltpu.VMEM, pltpu.SemaphoreType.DMA
    in_vmem = pl.BlockSpec(memory_space=pltpu.VMEM)
    in_smem = pl.BlockSpec(memory_space=pltpu.SMEM)
    anywhere = pl.BlockSpec(memory_space=pl.ANY)
    quads = task_dev // 4
    kv_new, grad_down, grad_up = pl.pallas_call(
        functools.partial(kernel, nz, nx, ny, most, width, kv, rank),
        out_shape=(
            jax.ShapeDtypeStruct((att, 2 * kv), bf16),
            jax.ShapeDtypeStruct((quads, 4 * rank, width), f32),
            jax.ShapeDtypeStruct((quads, 4 * rank, kv), f32),
        ),
        in_specs=[in_smem] * 2 + [in_vmem] * 3 + [anywhere] * 3,
        out_specs=(in_vmem, in_vmem, in_vmem),
        scratch_shapes=[
            pltpu.SMEM((groups,), i32),
            vmem(key_value_weight.shape, bf16),
            vmem((task_dev, rank, width), bf16),
            vmem((task_dev, rank, kv), bf16),
            vmem((groups, most, wide), bf16),
            vmem((groups, most, wide), bf16),
            vmem((groups, 1, 128), f32),
            vmem((groups, 1, 128), f32),
            vmem((att, 128), i32),
            vmem((groups, most, 128), f32),
            vmem((nx, 1, 2 * nz * most), i32),
            vmem((nx, 2, 2, nz // 2, most, kv), bf16),
            vmem((nx, 2, ny, most, 2 * rank), f32),
            vmem((nx, ny, most, 2 * rank), f32),
            vmem((nx, ny, most, 2 * rank), f32),
            vmem((nx, ny - 1, most, 2 * rank), f32),
            vmem((nx, most, 2 * rank), bf16),
            vmem((nx, tensors, most, 2 * rank), bf16),
            vmem((groups, most, 2 * kv), bf16),
            vmem((groups, most, 2 * kv), bf16),
            vmem((ny, att, 2 * kv), bf16),
            vmem((ny, att, 2 * kv), bf16),
            vmem((ny, att, 2 * kv), f32),
            vmem((ny, att, 2 * kv), bf16),
            vmem((ny, att, 2 * kv), bf16),
            dma((3,)),
            dma, dma((groups,)),
            dma, dma,
            dma, dma((nx,)),
            dma, dma((nx,)),
            dma, dma((nx,)),
            dma, dma,
            dma, dma,
            dma, dma,
        ],
        compiler_params=pltpu.CompilerParams(
            collective_id=0, has_side_effects=True, vmem_limit_bytes=52 << 20
        ),
    )(
        group_slot_task, task_row_position, attempt_adapter_slot.reshape(1, att),
        scores.reshape(1, att), rows_x,
        key_value_weight, jnp.swapaxes(adapter_down_weight, 1, 2), adapter_up_weight,
    )
    grad_down = (adapter_output_scale * grad_down).astype(bf16).reshape(task_dev, rank, width)
    grad_up = (adapter_output_scale * grad_up).astype(bf16).reshape(task_dev, rank, kv)
    return kv_new.reshape(att, steps, kv), jnp.swapaxes(grad_down, 1, 2), grad_up


def solution(mesh):
    in_specs = (
        P("dp", None, "tensor"),
        P("tensor", None),
        P("dp", "tensor", None),
        P("dp", None, "tensor"),
        P("dp", None),
        P(),
        P(),
        P("dp"),
        P("dp", None, "tensor"),
    )
    out_specs = (P("dp", None, "tensor"), P("dp", "tensor", None), P("dp", None, "tensor"))
    return jax.shard_map(
        functools.partial(body, 8, 32),
        mesh=mesh, in_specs=in_specs, out_specs=out_specs, check_vma=False,
    )
```

time: 210 us -> 122 us (0.58); the launches traced: 207 us -> 122 us
  Pallas kernels: 0 us -> 114 us
  waiting for transfers between devices: 63.4 us -> 0 us
  blocking collectives: 58.2 us -> 0 us
  starting transfers between devices: 31.6 us -> 0 us
  matrix products: 25.7 us -> 0 us
  between operations: 14.3 us -> 0.74 us
  local copies, waits for them, and re-layouts: 10.7 us -> 2.79 us
    pallas_call x0 -> x1, Pallas kernels: none -> 114 us  [body(): pl.pallas_call(functools.partial(kernel, nz, nx, ny, most, width, kv, ran...]
    all_to_all x4 -> x0, waiting for transfers between devices: 63.4 us -> none  [swap(): return lax.all_to_all(x, 'dp', split_axis=0, concat_axis=0, tiled=True)]
    psum x1 -> x0, blocking collectives: 58.2 us -> none  [body(): lax.psum(jnp.concatenate([inner_down, inner_back], axis=3), 'tensor')]
    all_to_all x4 -> x0, starting transfers between devices: 31.5 us -> none  [swap(): return lax.all_to_all(x, 'dp', split_axis=0, concat_axis=0, tiled=True)]
    dot_general x9 -> x0, matrix products: 25.7 us -> none  [the longest x1 7.05 us: body(): jnp.einsum('gjsd,gjstr->tdr', hid, spread, preferred_element_type=f32)]
    convert_element_type x2, other arithmetic: 0.08 us -> 3.58 us  [the longest x1 2.83 us: body(): (adapter_output_scale * grad_down).astype(bf16)]
    gather x2 -> x0, local copies, waits for them, and re-layouts: 3.5 us -> none  [the longest x1 2.07 us: body(): down = jnp.take(adapter_down_weight, local, axis=0)]
  transfers between devices with their start and end apart: 5 -> 0, of which waited for: 4 -> 0; matrix products, arithmetic and copies ran while one was open for 15% -> 0% of each run, Pallas kernels for 0% -> 0%
where the time goes in v3:
time: 122 us
  Pallas kernels  114 us (93%)
  other arithmetic  3.62 us (3%)
  local copies, waits for them, and re-layouts  2.79 us (2%)
    pallas_call x1, Pallas kernels, body(): pl.pallas_call(functools.partial(kernel, nz, nx, ny, most, width, kv, ran...  114 us
    convert_element_type x1, other arithmetic, body(): (adapter_output_scale * grad_down).astype(bf16)  2.83 us

profile of v3, /device:TPU:6, one launch (start us, length us, event | category | flops | bytes accessed | tf_op | source)
XLA Modules:
  0.0 121.6 jit_solution(16614900544373718829)
XLA Ops:
  0.6 0.0 copy-start.4
  0.6 0.0 copy-start.2
  0.7 0.0 copy-start.1
  0.7 0.0 copy-start.3
  0.7 0.0 copy-start
  0.7 1.0 copy.15
  1.7 1.1 copy.12
  2.8 0.0 copy-done.4
  2.8 0.0 copy-done.2
  2.8 0.0 copy-done.1
  2.9 0.0 copy-done.3
  2.9 0.0 copy-done
  2.9 114.4 %shard_map.112 = (bf16[256,256]{1,0:T(8,128)(2,1)S(1)}, f32[4,256,512]{2,1,0:T(8,128)}, f32[4,256,128]{2,1,0:T(8,128)S(1)}) custom-call(s32[32,32]{1,0:T(8,128)S(1)} %copy-done.1, s32[512]{0:T(512)S(1)} %copy-done.2, s32[1,256]{1,0:T(1,128)S(1)} %bitcast.13, s32[1,256]{1,0:T(1,128)S(1)} %bitcast.14, bf16[256,1280]{1,0:T(8,128)(2,1)S(1)} %pad_maximum_fusion.rows_x, ...), custom_call_target="tpu_custom_call" | custom-call | tf_op jit(solution)/shard_map/pallas_call | solution.py:380
  117.3 0.7 reshape.31
  118.0 0.7 multiply_convert_fusion.1
  118.8 2.8 %multiply_convert_fusion = bf16[4,256,512]{2,1,0:T(8,128)(2,1)} fusion(f32[4,256,512]{2,1,0:T(8,128)} %get-tuple-element.7), kind=kLoop, calls=%fused_computation | loop fusion | flops 1048576 | bytes 3145728 | tf_op jit(solution)/shard_map/convert_element_type | solution.py:433
  (1 shorter events, 0.0 us)
Async XLA Ops:
  0.6 2.2 %copy-start.4 = (s32[256]{0:T(256)S(1)}, s32[256]{0:T(256)}, u32[]{:S(2)}) copy-start(s32[256]{0:T(256)} %param.16) | copy-start | bytes 3076
  0.6 2.2 %copy-start.2 = (s32[512]{0:T(512)S(1)}, s32[512]{0:T(512)}, u32[]{:S(2)}) copy-start(s32[512]{0:T(512)} %task_row.1) | copy-start | bytes 6148
  0.7 2.2 %copy-start.1 = (s32[32,32]{1,0:T(8,128)S(1)}, s32[32,32]{1,0:T(8,128)}, u32[]{:S(2)}) copy-start(s32[32,32]{1,0:T(8,128)} %slot_task.1) | copy-start | bytes 12292
  0.7 2.2 %copy-start.3 = (s32[256,1]{0,1:T(1,128)S(1)}, s32[256,1]{0,1:T(1,128)}, u32[]{:S(2)}) copy-start(s32[256,1]{0,1:T(1,128)} %param.13) | copy-start | bytes 3076
  0.7 2.2 %copy-start = (bf16[16,64,128]{2,1,0:T(8,128)(2,1)S(1)}, bf16[16,64,128]{2,1,0:T(8,128)(2,1)}, u32[]{:S(2)}) copy-start(bf16[16,64,128]{2,1,0:T(8,128)(2,1)} %up_hbm.1) | copy-start | bytes 786436

commit v4 on v3

--- a/solution.py
+++ b/solution.py
@@ -311,13 +311,18 @@
     for c in range(nx):
         inner_parts(c)
         pair_copy(c).start()
+        if c > 0:
+            gather(c - 1)
         scatter(c)
-        if c > 0:
-            gradients(c - 1)
-        gather(c)
         if c + 1 < len(base_steps):
             spread_base(base_steps[c + 1])
-        deltas(c)
+        if c > 1:
+            gradients(c - 2)
+        if c > 0:
+            deltas(c - 1)
+    gather(nx - 1)
+    gradients(nx - 2)
+    deltas(nx - 1)
     gradients(nx - 1)
 
     base_wait = remote(

time: 122 us -> 114 us (0.934)
  Pallas kernels: 114 us -> 106 us
    pallas_call x1, Pallas kernels: 114 us -> 106 us  [body(): pl.pallas_call(functools.partial(kernel, nz, nx, ny, most, width, kv, ran...]
where the time goes in v4:
time: 114 us; the launch traced here: 113 us
  Pallas kernels  106 us (93%)
  other arithmetic  3.62 us (3%)
  local copies, waits for them, and re-layouts  2.79 us (2%)
    pallas_call x1, Pallas kernels, body(): pl.pallas_call(functools.partial(kernel, nz, nx, ny, most, width, kv, ran...  106 us
    convert_element_type x1, other arithmetic, body(): (adapter_output_scale * grad_down).astype(bf16)  2.83 us

profile of v4, /device:TPU:6, one launch (start us, length us, event | category | flops | bytes accessed | tf_op | source)
XLA Modules:
  0.0 113.2 jit_solution(16025125723722668895)
XLA Ops:
  0.6 0.0 copy-start.4
  0.6 0.0 copy-start.2
  0.7 0.0 copy-start.1
  0.7 0.0 copy-start.3
  0.7 0.0 copy-start
  0.7 1.0 copy.15
  1.7 1.1 copy.12
  2.8 0.0 copy-done.4
  2.8 0.0 copy-done.2
  2.8 0.0 copy-done.1
  2.9 0.0 copy-done.3
  2.9 0.0 copy-done
  2.9 106.1 %shard_map.112 = (bf16[256,256]{1,0:T(8,128)(2,1)S(1)}, f32[4,256,512]{2,1,0:T(8,128)}, f32[4,256,128]{2,1,0:T(8,128)S(1)}) custom-call(s32[32,32]{1,0:T(8,128)S(1)} %copy-done.1, s32[512]{0:T(512)S(1)} %copy-done.2, s32[1,256]{1,0:T(1,128)S(1)} %bitcast.13, s32[1,256]{1,0:T(1,128)S(1)} %bitcast.14, bf16[256,1280]{1,0:T(8,128)(2,1)S(1)} %pad_maximum_fusion.rows_x, ...), custom_call_target="tpu_custom_call" | custom-call | tf_op jit(solution)/shard_map/pallas_call | solution.py:385
  108.9 0.7 reshape.31
  109.6 0.7 multiply_convert_fusion.1
  110.4 2.8 %multiply_convert_fusion = bf16[4,256,512]{2,1,0:T(8,128)(2,1)} fusion(f32[4,256,512]{2,1,0:T(8,128)} %get-tuple-element.7), kind=kLoop, calls=%fused_computation | loop fusion | flops 1048576 | bytes 3145728 | tf_op jit(solution)/shard_map/convert_element_type | solution.py:438
  (1 shorter events, 0.0 us)
Async XLA Ops:
  0.6 2.2 %copy-start.4 = (s32[256]{0:T(256)S(1)}, s32[256]{0:T(256)}, u32[]{:S(2)}) copy-start(s32[256]{0:T(256)} %param.16) | copy-start | bytes 3076
  0.6 2.2 %copy-start.2 = (s32[512]{0:T(512)S(1)}, s32[512]{0:T(512)}, u32[]{:S(2)}) copy-start(s32[512]{0:T(512)} %task_row.1) | copy-start | bytes 6148
  0.7 2.2 %copy-start.1 = (s32[32,32]{1,0:T(8,128)S(1)}, s32[32,32]{1,0:T(8,128)}, u32[]{:S(2)}) copy-start(s32[32,32]{1,0:T(8,128)} %slot_task.1) | copy-start | bytes 12292
  0.7 2.2 %copy-start.3 = (s32[256,1]{0,1:T(1,128)S(1)}, s32[256,1]{0,1:T(1,128)}, u32[]{:S(2)}) copy-start(s32[256,1]{0,1:T(1,128)} %param.13) | copy-start | bytes 3076
  0.7 2.2 %copy-start = (bf16[16,64,128]{2,1,0:T(8,128)(2,1)S(1)}, bf16[16,64,128]{2,1,0:T(8,128)(2,1)}, u32[]{:S(2)}) copy-start(bf16[16,64,128]{2,1,0:T(8,128)(2,1)} %up_hbm.1) | copy-start | bytes 786436

commit v5 on v3

--- a/solution.py
+++ b/solution.py
@@ -27,11 +27,10 @@
 
 
 def kernel(
-    nz, nx, ny, most, width, kv, rank,
+    nz, nx, ny, most, width, kv, rank, steps_z, chunks,
     slot_task, task_row, slot, scores, rows_x, w_hbm, down_hbm, up_hbm,
     kv_out, acc_d, acc_u,
-    tau, w, down, up, sbuf, rbuf, marks, marks_in, places, adv, tau_lane, wbuf, part, pair_in, pair,
-    rs_in, ag_out, ag_in, dout, din, base_a, base_b, base_own, base_send, base_in,
+    tau, w, down, up, sbuf, rbuf, marks, marks_in, places, adv, tau_lane, wbuf, totals, dout, din, base_a, base_b, base_own, base_send, base_in,
     load_sem, rows_s, rows_r, marks_s, marks_r, pair_s, pair_r, rs_s, rs_r, ag_s, ag_r,
     del_s, del_r, ba_s, ba_r, by_s, by_r,
 ):
@@ -43,14 +42,15 @@
     mz, mx = lax.div(me, nx), lax.rem(me, nx)
     my, core = lax.div(mt, 2), lax.rem(mt, 2)
     sibling = mt + 1 - 2 * core
-    own = (nx - 1) * nz
+    own = (nx - 1) * nz + steps_z.index(0)
+    thin = most // 2
     span = nz * most
 
     def target(c, u):
-        return lax.rem(mz + u, nz) * nx + lax.rem(mx + c + 1, nx)
+        return lax.rem(mz + steps_z[u], nz) * nx + lax.rem(mx + c + 1, nx)
 
     def origin(c, u):
-        return lax.rem(mz + nz - u, nz) * nx + lax.rem(mx + 2 * nx - c - 1, nx)
+        return lax.rem(mz + nz - steps_z[u], nz) * nx + lax.rem(mx + 2 * nx - c - 1, nx)
 
     def remote(src, dst, s, r, dp, tensor):
         return pltpu.make_async_remote_copy(
@@ -90,7 +90,9 @@
     rank_row = jnp.sum(jnp.where(earlier, 1.0, 0.0), axis=0, keepdims=True)
     off_z = lax.rem(lax.div(slot_row, nx) + nz - mz, nz)
     off_x = lax.rem(lax.rem(slot_row, nx) + 2 * nx - mx - 1, nx)
-    k_row = off_x * nz + off_z
+    k_row = off_x * nz
+    for u in range(nz):
+        k_row = k_row + jnp.where(off_z == steps_z[u], u, 0)
     place_row = (k_row * most).astype(f32) + rank_row
     place_col = jnp.sum(jnp.where(diagonal, place_row, 0.0), axis=1, keepdims=True).astype(i32)
     place_row = place_row.astype(i32)
@@ -101,10 +103,10 @@
         out = dot(hot, rows_x[...]).astype(bf16).reshape(nz, most, rows_x.shape[1])
         sbuf[c * nz : (c + 1) * nz] = out
         if c == nx - 1:
-            rbuf[own] = out[0]
+            rbuf[own] = out[own % nz]
 
     def send_rows(c):
-        for u in sorted(range(nz), key=lambda d: -min(d, nz - d)):
+        for u in range(nz):
             k = c * nz + u
             if k != own:
                 remote(sbuf.at[k], rbuf.at[k], rows_s, rows_r.at[k], target(c, u), mt).start()
@@ -137,13 +139,11 @@
             tau[k] = task
             by_row = jnp.where(row == k, task, by_row)
             by_lane = jnp.where(lane == k, task, by_lane)
-        lane = iota((1, 2 * span), 1)
-        place = lax.div(lane, span) * half + lax.rem(lax.div(lane, most), half)
-        for c in range(nx):
-            line = jnp.zeros((1, 2 * span), i32)
-            for u in range(nz):
-                line = jnp.where(place == u, tau[c * nz + u], line)
-            tau_lane[c] = line
+        place = lax.div(iota((1, groups * most), 1), most)
+        line = jnp.zeros((1, groups * most), i32)
+        for k in range(groups):
+            line = jnp.where(place == k, tau[k], line)
+        tau_lane[...] = line
         return jnp.where(by_row == by_lane, 1.0, 0.0)
 
     def advantages(same):
@@ -190,96 +190,111 @@
             base_send[y] = (base_own[y] + base_b[y].astype(f32)).astype(bf16)
             remote(base_send.at[y], base_in.at[i], by_s, by_r, me, 2 * y + core).start()
 
-    def inner_parts(c):
-        for u in range(nz):
-            k, h, q = c * nz + u, u // half, u % half
+    def parts_of(i):
+        first, count = chunks[i]
+        return [(t, q, (first + t) * half + q) for t in range(count) for q in range(half)]
+
+    def inner_parts(i):
+        part = totals[i][0]
+        for t, q, k in parts_of(i):
             if k != own:
-                remote(sbuf.at[k], rbuf.at[k], rows_s, rows_r.at[k], origin(c, u), mt).wait_recv()
+                remote(
+                    sbuf.at[k], rbuf.at[k], rows_s, rows_r.at[k], origin(k // nz, k % nz), mt
+                ).wait_recv()
             task = tau[k]
             for s in range(2):
                 cot = rbuf[k, :, 2 * width + s * kv : 2 * width + (s + 1) * kv].astype(f32)
-                wbuf[c, h, s, q] = (adv[k][:, :kv] * cot).astype(bf16)
+                wbuf[s, k] = (adv[k][:, :kv] * cot).astype(bf16)
             both = jnp.concatenate([rbuf[k, :, :width], rbuf[k, :, width : 2 * width]], axis=0)
-            heavy = jnp.concatenate([wbuf[c, h, 0, q], wbuf[c, h, 1, q]], axis=0)
+            heavy = jnp.concatenate([wbuf[0, k], wbuf[1, k]], axis=0)
             inner = jnp.concatenate([dot_nt(both, down[task]), dot_nt(heavy, up[task])], axis=1)
-            part[c, h, q] = inner[:most]
-            part[c, h, half + q] = inner[most:]
-
-    def pair_copy(c):
-        return remote(part.at[c, 1 - core], pair_in.at[c], pair_s, pair_r.at[c], me, sibling)
-
-    def scatter(c):
-        pair_copy(c).wait_recv()
-        pair[c] = part[c, core] + pair_in[c]
-
-        def one(i, _):
-            y = lax.rem(my + i, ny)
+            for s in range(2):
+                for h in range(2):
+                    at = s * most + h * thin
+                    part[h, s * half + q, t] = inner[at : at + thin]
+
+    def pair_copy(i):
+        part, pair_in = totals[i][:2]
+        return remote(part.at[1 - core], pair_in, pair_s.at[i], pair_r.at[i], me, sibling)
+
+    def rs_wait(i):
+        _, _, pair, rs_in = totals[i][:4]
+        return remote(peers(pair, ny - 1), rs_in, rs_s.at[i], rs_r.at[i], me, sibling)
+
+    def ag_wait(i):
+        every = peers(totals[i][5], tensors - 1)
+        return remote(every, every, ag_s.at[i], ag_r.at[i], me, sibling)
+
+    def scatter(i):
+        part, pair_in, pair, rs_in = totals[i][:4]
+        pair_copy(i).wait_recv()
+        pair[...] = part[core] + pair_in[...]
+        for step in range(1, ny):
+            y = lax.rem(my + step, ny)
             remote(
-                pair.at[c, y], rs_in.at[c, i - 1], rs_s, rs_r.at[c], me, 2 * y + core
+                pair.at[y], rs_in.at[step - 1], rs_s.at[i], rs_r.at[i], me, 2 * y + core
             ).start()
+
+    def gather(i):
+        _, _, pair, rs_in, ag_out, ag_in = totals[i]
+        rs_wait(i).wait_recv()
+        total = pair[my]
+        for step in range(ny - 1):
+            total = total + rs_in[step]
+        piece = core * ny + my
+        ag_out[...] = total.astype(bf16)
+        ag_in[piece] = total.astype(bf16)
+
+        def one(step, _):
+            to = lax.rem(mt + step, tensors)
+            remote(ag_out, ag_in.at[piece], ag_s.at[i], ag_r.at[i], me, to).start()
             return 0
 
-        lax.fori_loop(1, ny, one, 0)
-
-    def gather(c):
-        remote(
-            peers(pair.at[c], ny - 1), rs_in.at[c], rs_s, rs_r.at[c], me, sibling
-        ).wait_recv()
-        total = pair[c, my]
-        for i in range(ny - 1):
-            total = total + rs_in[c, i]
-        piece = core * ny + my
-        ag_out[c] = total.astype(bf16)
-        ag_in[c, piece] = total.astype(bf16)
-
-        def one(i, _):
-            to = lax.rem(mt + i, tensors)
-            remote(ag_out.at[c], ag_in.at[c, piece], ag_s, ag_r.at[c], me, to).start()
-            return 0
-
         lax.fori_loop(1, tensors, one, 0)
 
-    def deltas(c):
-        remote(
-            peers(ag_in.at[c], tensors - 1), peers(ag_in.at[c], tensors - 1), ag_s, ag_r.at[c],
-            me, sibling,
-        ).wait_recv()
-        for u in range(nz):
-            k, h, q = c * nz + u, u // half, u % half
-            inner = jnp.concatenate([ag_in[c, h * ny + q], ag_in[c, h * ny + half + q]], axis=0)
+    def deltas(i):
+        ag_in = totals[i][5]
+        ag_wait(i).wait_recv()
+        for t, q, k in parts_of(i):
+            inner = jnp.concatenate(
+                [ag_in[h * ny + s * half + q, t] for s in range(2) for h in range(2)], axis=0
+            )
             delta = (adapter_output_scale * dot(inner[:, :rank], up[tau[k]])).astype(bf16)
             delta = jnp.concatenate([delta[:most], delta[most:]], axis=1)
             if k == own:
                 din[k] = delta
             else:
                 dout[k] = delta
-                remote(dout.at[k], din.at[k], del_s, del_r, origin(c, u), mt).start()
-
-    def gradients(c):
-        inner = ag_in[c].reshape(tensors * most, 2 * rank).astype(f32).T
+                remote(
+                    dout.at[k], din.at[k], del_s, del_r, origin(k // nz, k % nz), mt
+                ).start()
+
+    def gradients(i):
+        ag_in = totals[i][5]
+        first, last = chunks[i][0] * half, (chunks[i][0] + chunks[i][1]) * half
+        rows_n = (last - first) * most
+        inner = jnp.concatenate(
+            [
+                ag_in[h * ny + s * half + q, t]
+                for s in range(2)
+                for t, q, _ in parts_of(i)
+                for h in range(2)
+            ],
+            axis=0,
+        )
+        inner = inner.astype(f32).T
         inner_d, inner_b = inner[:rank].astype(bf16), inner[rank:].astype(bf16)
-        task_lane = tau_lane[c]
-        weighted = wbuf[c].reshape(2 * span, kv)
+        line = tau_lane[:, first * most : last * most]
+        line = jnp.concatenate([line, line], axis=1)
+        weighted = wbuf[:, first:last].reshape(2 * rows_n, kv)
 
         def one(g, _):
-            hots = [
-                jnp.where(task_lane == g * some + i, 1.0, 0.0).astype(bf16) for i in range(some)
-            ]
+            hots = [jnp.where(line == g * some + j, 1.0, 0.0).astype(bf16) for j in range(some)]
             spread = jnp.concatenate([inner_b * hot for hot in hots], axis=0)
             terms = acc_d[g]
-            for h in range(2):
-                rows = jnp.concatenate(
-                    [
-                        rbuf[
-                            c * nz + h * half : c * nz + (h + 1) * half,
-                            :,
-                            s * width : (s + 1) * width,
-                        ].reshape(half * most, width)
-                        for s in range(2)
-                    ],
-                    axis=0,
-                )
-                terms = terms + dot(spread[:, h * span : (h + 1) * span], rows)
+            for s in range(2):
+                rows = rbuf[first:last, :, s * width : (s + 1) * width].reshape(rows_n, width)
+                terms = terms + dot(spread[:, s * rows_n : (s + 1) * rows_n], rows)
             acc_d[g] = terms
             spread = jnp.concatenate([inner_d * hot for hot in hots], axis=0)
             acc_u[g] += dot(spread, weighted)
@@ -288,10 +303,10 @@
         lax.fori_loop(0, acc_d.shape[0], one, 0)
 
     bucket(0)
+    pl.semaphore_wait(barrier, groups - 1 + tensors - 1)
+    send_rows(0)
     make_marks()
-    pl.semaphore_wait(barrier, groups - 1 + tensors - 1)
     send_marks()
-    send_rows(0)
     for c in range(1, nx):
         bucket(c)
         send_rows(c)
@@ -308,17 +323,23 @@
     advantages(same)
     loads[1].wait()
     loads[2].wait()
-    for c in range(nx):
-        inner_parts(c)
-        pair_copy(c).start()
-        scatter(c)
-        if c > 0:
-            gradients(c - 1)
-        gather(c)
-        if c + 1 < len(base_steps):
-            spread_base(base_steps[c + 1])
-        deltas(c)
-    gradients(nx - 1)
+    final = len(chunks) - 1
+    for i in range(final + 1):
+        inner_parts(i)
+        pair_copy(i).start()
+        if i > 0:
+            gather(i - 1)
+        scatter(i)
+        if i + 1 < len(base_steps):
+            spread_base(base_steps[i + 1])
+        if i > 1:
+            gradients(i - 2)
+        if i > 0:
+            deltas(i - 1)
+    gather(final)
+    gradients(final - 1)
+    deltas(final)
+    gradients(final)
 
     base_wait = remote(
         peers(base_send, ny - 1), peers(base_in, ny - 1), by_s, by_r, me, sibling
@@ -344,10 +365,10 @@
     exchange.wait_send()
     base_wait.wait_send()
     delta_wait.wait_send()
-    remote(pair_in, pair_in, pair_s, pair_r.at[0], me, sibling).wait_send()
-    remote(rs_in, rs_in, rs_s, rs_r.at[0], me, sibling).wait_send()
-    sent = ag_in.at[:, pl.ds(0, tensors - 1)]
-    remote(sent, sent, ag_s, ag_r.at[0], me, sibling).wait_send()
+    for i in range(final + 1):
+        pair_copy(i).wait_send()
+        rs_wait(i).wait_send()
+        ag_wait(i).wait_send()
 
 
 def body(
@@ -377,8 +398,24 @@
     in_smem = pl.BlockSpec(memory_space=pltpu.SMEM)
     anywhere = pl.BlockSpec(memory_space=pl.ANY)
     quads = task_dev // 4
+    steps_z = (3, 5, 2, 6, 4, 0, 1, 7) if nz == 8 else tuple(range(1, nz)) + (0,)
+    units = 2 * nx
+    chunks = tuple((i, 2) for i in range(0, units, 2))
+    totals = []
+    for _, count in chunks:
+        piece = (count, most // 2, 2 * rank)
+        totals.append(
+            (
+                vmem((2, ny) + piece, f32),
+                vmem((ny,) + piece, f32),
+                vmem((ny,) + piece, f32),
+                vmem((ny - 1,) + piece, f32),
+                vmem(piece, bf16),
+                vmem((2 * ny,) + piece, bf16),
+            )
+        )
     kv_new, grad_down, grad_up = pl.pallas_call(
-        functools.partial(kernel, nz, nx, ny, most, width, kv, rank),
+        functools.partial(kernel, nz, nx, ny, most, width, kv, rank, steps_z, chunks),
         out_shape=(
             jax.ShapeDtypeStruct((att, 2 * kv), bf16),
             jax.ShapeDtypeStruct((quads, 4 * rank, width), f32),
@@ -397,14 +434,9 @@
             vmem((groups, 1, 128), f32),
             vmem((att, 128), i32),
             vmem((groups, most, 128), f32),
-            vmem((nx, 1, 2 * nz * most), i32),
-            vmem((nx, 2, 2, nz // 2, most, kv), bf16),
-            vmem((nx, 2, ny, most, 2 * rank), f32),
-            vmem((nx, ny, most, 2 * rank), f32),
-            vmem((nx, ny, most, 2 * rank), f32),
-            vmem((nx, ny - 1, most, 2 * rank), f32),
-            vmem((nx, most, 2 * rank), bf16),
-            vmem((nx, tensors, most, 2 * rank), bf16),
+            vmem((1, groups * most), i32),
+            vmem((2, groups, most, kv), bf16),
+            totals,
             vmem((groups, most, 2 * kv), bf16),
             vmem((groups, most, 2 * kv), bf16),
             vmem((ny, att, 2 * kv), bf16),
@@ -415,15 +447,15 @@
             dma((3,)),
             dma, dma((groups,)),
             dma, dma,
-            dma, dma((nx,)),
-            dma, dma((nx,)),
-            dma, dma((nx,)),
+            dma((len(chunks),)), dma((len(chunks),)),
+            dma((len(chunks),)), dma((len(chunks),)),
+            dma((len(chunks),)), dma((len(chunks),)),
             dma, dma,
             dma, dma,
             dma, dma,
         ],
         compiler_params=pltpu.CompilerParams(
-            collective_id=0, has_side_effects=True, vmem_limit_bytes=52 << 20
+            collective_id=0, has_side_effects=True, vmem_limit_bytes=36 << 20
         ),
     )(
         group_slot_task, task_row_position, attempt_adapter_slot.reshape(1, att),

time: 122 us -> 105 us (0.86)
  Pallas kernels: 114 us -> 98.4 us
  other arithmetic: 3.62 us -> 2.03 us
  local copies, waits for them, and re-layouts: 2.79 us -> 4.12 us
    pallas_call x1, Pallas kernels: 114 us -> 98.4 us  [body(): pl.pallas_call(functools.partial(kernel, nz, nx, ny, most, width, kv, ran...]
    convert_element_type x1, other arithmetic: 2.83 us -> 1.24 us  [body(): (adapter_output_scale * grad_down).astype(bf16)]
    unnamed x12 -> x16, local copies, waits for them, and re-layouts: 2.1 us -> 3.43 us
where the time goes in v5:
time: 105 us
  Pallas kernels  98.4 us (94%)
  local copies, waits for them, and re-layouts  4.12 us (4%)
  other arithmetic  2.03 us (2%)
    pallas_call x1, Pallas kernels, body(): pl.pallas_call(functools.partial(kernel, nz, nx, ny, most, width, kv, ran...  98.4 us
    unnamed x16, local copies, waits for them, and re-layouts  3.43 us

profile of v5, /device:TPU:6, one launch (start us, length us, event | category | flops | bytes accessed | tf_op | source)
XLA Modules:
  0.0 105.3 jit_solution(4311926472523656384)
XLA Ops:
  0.6 0.0 copy-start.6
  0.6 0.0 copy-start.4
  0.7 0.0 copy-start.3
  0.7 0.0 copy-start.5
  0.7 0.0 copy-start.2
  0.7 0.0 copy-start
  0.7 1.1 %copy.15 = bf16[32,8,2,128]{3,1,2,0:T(8,128)(2,1)S(1)} copy(bf16[32,8,2,128]{3,2,1,0:T(2,128)(2,1)} %bitcast.21) | data formatting | bytes 262144
  1.8 1.1 %copy.12 = bf16[32,8,2,512]{3,1,2,0:T(8,128)(2,1)S(1)} copy(bf16[32,8,2,512]{3,2,1,0:T(2,128)(2,1)} %bitcast.19) | data formatting | bytes 1048576
  2.9 0.0 copy-done.6
  2.9 0.0 copy-done.4
  3.0 0.0 copy-done.3
  3.0 0.0 copy-done.5
  3.0 0.0 copy-done.2
  3.0 0.0 copy-done
  3.0 0.0 copy-start.1
  3.0 1.2 %copy-done.1 = bf16[16,512,64]{1,2,0:T(8,128)(2,1)S(1)} copy-done((bf16[16,512,64]{1,2,0:T(8,128)(2,1)S(1)}, bf16[16,512,64]{1,2,0:T(8,128)(2,1)}, u32[]{:S(2)}) %copy-start.1) | copy-done | bytes 1048600
  4.2 98.4 %shard_map.112 = (bf16[256,256]{1,0:T(8,128)(2,1)S(1)}, f32[4,256,512]{2,1,0:T(8,128)S(1)}, f32[4,256,128]{2,1,0:T(8,128)S(1)}) custom-call(s32[32,32]{1,0:T(8,128)S(1)} %copy-done.3, s32[512]{0:T(512)S(1)} %copy-done.4, s32[1,256]{1,0:T(1,128)S(1)} %bitcast.14, s32[1,256]{1,0:T(1,128)S(1)} %bitcast.15, bf16[256,1280]{1,0:T(8,128)(2,1)S(1)} %pad_maximum_fusion.rows_x, ...), custom_call_target="tpu_custom_call" | custom-call | tf_op jit(solution)/shard_map/pallas_call | solution.py:417
  102.6 0.7 reshape.31
  103.3 0.7 multiply_convert_fusion.1
  104.0 1.2 %multiply_convert_fusion = bf16[4,256,512]{2,1,0:T(8,128)(2,1)} fusion(f32[4,256,512]{2,1,0:T(8,128)S(1)} %get-tuple-element.7), kind=kLoop, calls=%fused_computation | loop fusion | flops 1048576 | bytes 3145728 | tf_op jit(solution)/shard_map/convert_element_type | solution.py:465
  (1 shorter events, 0.0 us)
Async XLA Ops:
  0.6 2.3 %copy-start.6 = (s32[256]{0:T(256)S(1)}, s32[256]{0:T(256)}, u32[]{:S(2)}) copy-start(s32[256]{0:T(256)} %param.16) | copy-start | bytes 3076
  0.6 2.3 %copy-start.4 = (s32[512]{0:T(512)S(1)}, s32[512]{0:T(512)}, u32[]{:S(2)}) copy-start(s32[512]{0:T(512)} %task_row.1) | copy-start | bytes 6148
  0.7 2.3 %copy-start.3 = (s32[32,32]{1,0:T(8,128)S(1)}, s32[32,32]{1,0:T(8,128)}, u32[]{:S(2)}) copy-start(s32[32,32]{1,0:T(8,128)} %slot_task.1) | copy-start | bytes 12292
  0.7 2.3 %copy-start.5 = (s32[256,1]{0,1:T(1,128)S(1)}, s32[256,1]{0,1:T(1,128)}, u32[]{:S(2)}) copy-start(s32[256,1]{0,1:T(1,128)} %param.13) | copy-start | bytes 3076
  0.7 2.3 %copy-start.2 = (bf16[16,64,128]{2,1,0:T(8,128)(2,1)S(1)}, bf16[16,64,128]{2,1,0:T(8,128)(2,1)}, u32[]{:S(2)}) copy-start(bf16[16,64,128]{2,1,0:T(8,128)(2,1)} %up_hbm.1) | copy-start | bytes 786436
  0.7 2.3 %copy-start = (bf16[512,2048]{1,0:T(8,128)(2,1)S(1)}, bf16[512,2048]{1,0:T(8,128)(2,1)}, u32[]{:S(2)}) copy-start(bf16[512,2048]{1,0:T(8,128)(2,1)} %w_hbm.1) | copy-start | bytes 6291460
  3.0 1.2 %copy-start.1 = (bf16[16,512,64]{1,2,0:T(8,128)(2,1)S(1)}, bf16[16,512,64]{1,2,0:T(8,128)(2,1)}, u32[]{:S(2)}) copy-start(bf16[16,512,64]{1,2,0:T(8,128)(2,1)} %param.11) | copy-start | bytes 3145732

commit v6 on v5

--- a/solution.py
+++ b/solution.py
@@ -266,7 +266,7 @@
             else:
                 dout[k] = delta
                 remote(
-                    dout.at[k], din.at[k], del_s, del_r, origin(k // nz, k % nz), mt
+                    dout.at[k], din.at[k], del_s.at[i], del_r.at[i], origin(k // nz, k % nz), mt
                 ).start()
 
     def gradients(i):
@@ -348,13 +348,21 @@
     total = base_own[my] + base_b[my].astype(f32)
     for i in range(1, ny):
         total = total + base_in[i].astype(f32)
-    delta_wait = remote(
-        peers(dout, groups - 1), peers(din, groups - 1), del_s, del_r, me, sibling
-    )
-    delta_wait.wait_recv()
-    place = jnp.concatenate([places[...]] * (groups * most // 128), axis=1)
-    hot = jnp.where(iota((att, groups * most), 1) == place, 1.0, 0.0).astype(bf16)
-    kv_out[...] = (total + dot(hot, din[...].reshape(groups * most, 2 * kv))).astype(bf16)
+    def delta_wait(i):
+        count = sum(k != own for _, _, k in parts_of(i))
+        return remote(
+            peers(dout, count), peers(din, count), del_s.at[i], del_r.at[i], me, sibling
+        )
+
+    for i in range(final + 1):
+        first, count = chunks[i][0] * half, chunks[i][1] * half
+        lanes = iota((att, count * most), 1) + first * most
+        place = jnp.concatenate([places[...]] * pl.cdiv(count * most, 128), axis=1)
+        place = place[:, : count * most]
+        hot = jnp.where(lanes == place, 1.0, 0.0).astype(bf16)
+        delta_wait(i).wait_recv()
+        total = total + dot(hot, din[first : first + count].reshape(count * most, 2 * kv))
+    kv_out[...] = total.astype(bf16)
 
     remote(
         peers(sbuf, groups - 1), peers(rbuf, groups - 1), rows_s, rows_r.at[0], me, sibling
@@ -364,8 +372,8 @@
     ).wait_send()
     exchange.wait_send()
     base_wait.wait_send()
-    delta_wait.wait_send()
     for i in range(final + 1):
+        delta_wait(i).wait_send()
         pair_copy(i).wait_send()
         rs_wait(i).wait_send()
         ag_wait(i).wait_send()
@@ -396,7 +404,7 @@
     vmem, dma = pltpu.VMEM, pltpu.SemaphoreType.DMA
     in_vmem = pl.BlockSpec(memory_space=pltpu.VMEM)
     in_smem = pl.BlockSpec(memory_space=pltpu.SMEM)
-    anywhere = pl.BlockSpec(memory_space=pl.ANY)
+    anywhere = pl.BlockSpec(memory_space=pltpu.HBM)
     quads = task_dev // 4
     steps_z = (3, 5, 2, 6, 4, 0, 1, 7) if nz == 8 else tuple(range(1, nz)) + (0,)
     units = 2 * nx
@@ -450,7 +458,7 @@
             dma((len(chunks),)), dma((len(chunks),)),
             dma((len(chunks),)), dma((len(chunks),)),
             dma((len(chunks),)), dma((len(chunks),)),
-            dma, dma,
+            dma((len(chunks),)), dma((len(chunks),)),
             dma, dma,
             dma, dma,
         ],

time: 105 us -> 105 us (level)
  no operation moved by 1% of the time
where the time goes in v6:
time: 105 us
  Pallas kernels  98.3 us (94%)
  local copies, waits for them, and re-layouts  4.12 us (4%)
  other arithmetic  2.03 us (2%)
    pallas_call x1, Pallas kernels, body(): pl.pallas_call(functools.partial(kernel, nz, nx, ny, most, width, kv, ran...  98.3 us
    unnamed x16, local copies, waits for them, and re-layouts  3.43 us

profile of v6, /device:TPU:6, one launch (start us, length us, event | category | flops | bytes accessed | tf_op | source)
XLA Modules:
  0.0 105.2 jit_solution(12365581155171771904)
XLA Ops:
  0.6 0.0 copy-start.6
  0.6 0.0 copy-start.4
  0.7 0.0 copy-start.3
  0.7 0.0 copy-start.5
  0.7 0.0 copy-start.2
  0.7 0.0 copy-start
  0.7 1.1 %copy.15 = bf16[32,8,2,128]{3,1,2,0:T(8,128)(2,1)S(1)} copy(bf16[32,8,2,128]{3,2,1,0:T(2,128)(2,1)} %bitcast.21) | data formatting | bytes 262144
  1.8 1.1 %copy.12 = bf16[32,8,2,512]{3,1,2,0:T(8,128)(2,1)S(1)} copy(bf16[32,8,2,512]{3,2,1,0:T(2,128)(2,1)} %bitcast.19) | data formatting | bytes 1048576
  2.9 0.0 copy-done.6
  2.9 0.0 copy-done.4
  3.0 0.0 copy-done.3
  3.0 0.0 copy-done.5
  3.0 0.0 copy-done.2
  3.0 0.0 copy-done
  3.0 0.0 copy-start.1
  3.0 1.2 %copy-done.1 = bf16[16,512,64]{1,2,0:T(8,128)(2,1)S(1)} copy-done((bf16[16,512,64]{1,2,0:T(8,128)(2,1)S(1)}, bf16[16,512,64]{1,2,0:T(8,128)(2,1)}, u32[]{:S(2)}) %copy-start.1) | copy-done | bytes 1048600
  4.2 98.3 %shard_map.112 = (bf16[256,256]{1,0:T(8,128)(2,1)S(1)}, f32[4,256,512]{2,1,0:T(8,128)S(1)}, f32[4,256,128]{2,1,0:T(8,128)S(1)}) custom-call(s32[32,32]{1,0:T(8,128)S(1)} %copy-done.3, s32[512]{0:T(512)S(1)} %copy-done.4, s32[1,256]{1,0:T(1,128)S(1)} %bitcast.14, s32[1,256]{1,0:T(1,128)S(1)} %bitcast.15, bf16[256,1280]{1,0:T(8,128)(2,1)S(1)} %pad_maximum_fusion.rows_x, ...), custom_call_target="tpu_custom_call" | custom-call | tf_op jit(solution)/shard_map/pallas_call | solution.py:425
  102.5 0.7 reshape.31
  103.2 0.7 multiply_convert_fusion.1
  104.0 1.2 %multiply_convert_fusion = bf16[4,256,512]{2,1,0:T(8,128)(2,1)} fusion(f32[4,256,512]{2,1,0:T(8,128)S(1)} %get-tuple-element.7), kind=kLoop, calls=%fused_computation | loop fusion | flops 1048576 | bytes 3145728 | tf_op jit(solution)/shard_map/convert_element_type | solution.py:473
  (1 shorter events, 0.0 us)
Async XLA Ops:
  0.6 2.3 %copy-start.6 = (s32[256]{0:T(256)S(1)}, s32[256]{0:T(256)}, u32[]{:S(2)}) copy-start(s32[256]{0:T(256)} %param.16) | copy-start | bytes 3076
  0.6 2.3 %copy-start.4 = (s32[512]{0:T(512)S(1)}, s32[512]{0:T(512)}, u32[]{:S(2)}) copy-start(s32[512]{0:T(512)} %task_row.1) | copy-start | bytes 6148
  0.7 2.3 %copy-start.3 = (s32[32,32]{1,0:T(8,128)S(1)}, s32[32,32]{1,0:T(8,128)}, u32[]{:S(2)}) copy-start(s32[32,32]{1,0:T(8,128)} %slot_task.1) | copy-start | bytes 12292
  0.7 2.3 %copy-start.5 = (s32[256,1]{0,1:T(1,128)S(1)}, s32[256,1]{0,1:T(1,128)}, u32[]{:S(2)}) copy-start(s32[256,1]{0,1:T(1,128)} %param.13) | copy-start | bytes 3076
  0.7 2.3 %copy-start.2 = (bf16[16,64,128]{2,1,0:T(8,128)(2,1)S(1)}, bf16[16,64,128]{2,1,0:T(8,128)(2,1)}, u32[]{:S(2)}) copy-start(bf16[16,64,128]{2,1,0:T(8,128)(2,1)} %up_hbm.1) | copy-start | bytes 786436
  0.7 2.3 %copy-start = (bf16[512,2048]{1,0:T(8,128)(2,1)S(1)}, bf16[512,2048]{1,0:T(8,128)(2,1)}, u32[]{:S(2)}) copy-start(bf16[512,2048]{1,0:T(8,128)(2,1)} %w_hbm.1) | copy-start | bytes 6291460
  3.0 1.2 %copy-start.1 = (bf16[16,512,64]{1,2,0:T(8,128)(2,1)S(1)}, bf16[16,512,64]{1,2,0:T(8,128)(2,1)}, u32[]{:S(2)}) copy-start(bf16[16,512,64]{1,2,0:T(8,128)(2,1)} %param.11) | copy-start | bytes 3145732
